TPU v7x, 128 devices: a whole 4x4x4 slice. The times are simulated.
128 devices in a mesh: rows: 128 (over x, y, z, core).
Axes of the slice: x: 4, y: 4, z: 4, core: 2. Of those that a mesh axis runs over, the one named last changes fastest.
Arguments:
- stiffness: float32 [9, 512, 512], P(None, 'rows'), may hold values from -400 to 806.1, as said below
- mass: float32 [9, 512, 512], P(None, 'rows'), may hold values from 0.05 to 3, as said below
- shifts: float32 [3], replicated, may hold values from 0.05 to 2
- factor: float32 [512, 32, 512], P('rows'), may hold values from -6 to 6
Outputs:
- lowrank: float32 [3, 512, 32, 512], P(None, 'rows')
- residual_factor: float32 [512, 32, 512], P('rows')
Inputs may be any that keep to these rules, and one draw needn't show every extreme that they name: `stiffness`: entry 4 along the first dimension exceeds the sum of the magnitudes of the other eight, which are negative. `mass`: entry 4 along the first dimension exceeds the sum of the other eight, which are positive.
All inputs are finite; a program needn't handle non-finite values.
Results may differ from a plain program's by a relative error of at most 0.0003.
Values sent between devices are 32-bit elements; how exact they have to be, the bound alone decides.
A program may use at most 128 MiB of HBM per device.

v0:
```python
import functools

import jax
import jax.numpy as jnp
from jax import lax
from jax.experimental import pallas as pl
from jax.experimental.pallas import tpu as pltpu
from jax.sharding import PartitionSpec as P

STEPS = 3
ITERS = 4
MESH = pl.DeviceIdType.MESH
PAIRS = [(i, j) for i in range(ITERS + 1) for j in range(i, ITERS + 1)]
LANES = 128
CHUNK = 4
F32 = jnp.float32
BF16 = jnp.bfloat16

NAMES = ["w1", "w2", "i0", "i1", "i2", "c0", "c1", "a3", "c3", "e0", "e1", "e2", "f0", "f1", "f2", "inv"]
NAMES += ["al%d" % n for n in range(7)] + ["ga%d" % n for n in range(7)]
SLOT = {name: n for n, name in enumerate(NAMES)}
OFF = (0, 1, 2, 6, 7, 8)


def lane_roll(x, shift):
    return pltpu.roll(x, shift % LANES, axis=x.ndim - 1)


def split3(x):
    a = x.astype(BF16)
    rest = x - a.astype(F32)
    b = rest.astype(BF16)
    c = (rest - b.astype(F32)).astype(BF16)
    return a, b, c


def permuted(x, perm, dim):
    total = None
    for part in split3(x):
        term = lax.dot_general(part, perm, (((1,), (dim,)), ((), ())), preferred_element_type=F32)
        total = term if total is None else total + term
    return total


def line_factors(a, b, c):
    out = {}
    i0 = 1.0 / b[0]
    w1 = a[1] * i0
    i1 = 1.0 / (b[1] - w1 * c[0])
    w2 = a[2] * i1
    i2 = 1.0 / (b[2] - w2 * c[1])
    t1 = -w1 * a[0]
    e2 = -w2 * t1 * i2
    e1 = (t1 - c[1] * e2) * i1
    e0 = (a[0] - c[0] * e1) * i0
    f2 = c[2] * i2
    f1 = -c[1] * f2 * i1
    f0 = -c[0] * f1 * i0
    out.update(w1=w1, w2=w2, i0=i0, i1=i1, i2=i2, c0=c[0], c1=c[1], a3=a[3], c3=c[3])
    out.update(e0=e0, e1=e1, e2=e2, f0=f0, f1=f1, f2=f2)
    low = -a[3] * e2
    mid = b[3] - a[3] * f2 - c[3] * lane_roll(e0, -1)
    high = -c[3] * lane_roll(f0, -1)
    for level in range(7):
        k = 1 << level
        inv = 1.0 / mid
        al = -low * lane_roll(inv, k)
        ga = -high * lane_roll(inv, -k)
        mid = mid + al * lane_roll(high, k) + ga * lane_roll(low, -k)
        low, high = al * lane_roll(low, k), ga * lane_roll(high, -k)
        out["al%d" % level] = al
        out["ga%d" % level] = ga
    out["inv"] = 1.0 / mid
    return out


def least_squares(columns, initial):
    count = len(columns)
    cosines, sines = [], []
    rhs = [initial] + [None] * count
    upper = []
    for position in range(count):
        column = list(columns[position])
        for earlier in range(position):
            first = cosines[earlier] * column[earlier] + sines[earlier] * column[earlier + 1]
            second = -sines[earlier] * column[earlier] + cosines[earlier] * column[earlier + 1]
            column[earlier], column[earlier + 1] = first, second
        radius = jnp.sqrt(column[position] * column[position] + column[position + 1] * column[position + 1])
        inverse = 1.0 / radius
        cosine = column[position] * inverse
        sine = column[position + 1] * inverse
        cosines.append(cosine)
        sines.append(sine)
        rhs[position + 1] = -sine * rhs[position]
        rhs[position] = cosine * rhs[position]
        upper.append(column[:position] + [inverse])
    y = [None] * count
    for position in reversed(range(count)):
        accum = rhs[position]
        for onward in range(position + 1, count):
            accum = accum - upper[onward][position] * y[onward]
        y[position] = accum * upper[position][position]
    return y


def solve_weights(gram):
    n = ITERS + 1
    r = {}
    for i in range(n):
        pivot = gram[(i, i)]
        for m in range(i):
            pivot = pivot - r[(m, i)] * r[(m, i)]
        pivot = jnp.maximum(pivot, gram[(i, i)] * 1e-9)
        root = jnp.sqrt(pivot)
        r[(i, i)] = root
        inverse = 1.0 / root
        for j in range(i + 1, n):
            value = gram[(i, j)]
            for m in range(i):
                value = value - r[(m, i)] * r[(m, j)]
            r[(i, j)] = value * inverse
    columns = []
    for k in range(ITERS):
        columns.append([r[(i, k)] + r[(i, k + 1)] for i in range(k + 1)] + [r[(k + 1, k + 1)]])
    return least_squares(columns, r[(0, 0)])


def kernel(chips, shifts, stiff_hbm, mass_hbm, factor_hbm, low_hbm, res_hbm,
           perm, raw_s, raw_m, raw_w, lhs, ce, fc, pb, zb, ub, us, os_, arb, hx, msg,
           in_send, in_recv, far_send, ar_send, ar_recv, hx_send, hx_recv, out_send, out_recv, out_local):
    me = lax.axis_index("rows")
    k = me // 2
    c = me % 2
    up = lax.rem(k + chips - 1, chips)
    down = lax.rem(k + 1, chips)

    def device(chip, core):
        return (chip * 2 + core,)

    barrier = pltpu.get_barrier_semaphore()

    def greet(n, carry):
        pl.semaphore_signal(barrier, inc=1, device_id=device(lax.rem(k + n, chips), c), device_id_type=MESH)
        return carry

    for chip in (k, up, down):
        pl.semaphore_signal(barrier, inc=1, device_id=device(chip, 1 - c), device_id_type=MESH)
    lax.fori_loop(1, chips, greet, 0)

    own = 2 + c
    own_copies = [
        pltpu.make_async_copy(stiff_hbm, raw_s.at[own], in_recv.at[own, 0]),
        pltpu.make_async_copy(mass_hbm, raw_m.at[own], in_recv.at[own, 1]),
        pltpu.make_async_copy(factor_hbm.at[:, pl.ds(pl.multiple_of(16 * c, 16), 16), :], raw_w.at[own], in_recv.at[own, 2]),
    ]
    for copy in own_copies:
        copy.start()

    row = lax.broadcasted_iota(jnp.int32, (512, 512), 0)
    col = lax.broadcasted_iota(jnp.int32, (512, 512), 1)
    perm[...] = jnp.where(row == CHUNK * (col % LANES) + col // LANES, 1.0, 0.0).astype(BF16)

    pl.semaphore_wait(barrier, chips - 1 + 3)

    def block_copies(chip, core, block, sems):
        return [
            pltpu.make_async_remote_copy(
                src_ref=factor_hbm.at[:, pl.ds(pl.multiple_of(16 * core, 16), 16), :], dst_ref=raw_w.at[block],
                send_sem=sems.at[2], recv_sem=in_recv.at[block, 2], device_id=device(chip, core), device_id_type=MESH),
            pltpu.make_async_remote_copy(
                src_ref=stiff_hbm, dst_ref=raw_s.at[block],
                send_sem=sems.at[0], recv_sem=in_recv.at[block, 0], device_id=device(chip, core), device_id_type=MESH),
            pltpu.make_async_remote_copy(
                src_ref=mass_hbm, dst_ref=raw_m.at[block],
                send_sem=sems.at[1], recv_sem=in_recv.at[block, 1], device_id=device(chip, core), device_id_type=MESH),
        ]

    near_chip = lax.rem(k + 2 * c - 1 + chips, chips)
    far_chip = lax.rem(k + 1 - 2 * c + chips, chips)
    near_copies = []
    for core in range(2):
        near_copies += block_copies(near_chip, core, 4 - 3 * c, in_send.at[core])
    near_copies += block_copies(k, 1 - c, own, in_send.at[2])
    far_copies = []
    for core in range(2):
        far_copies += block_copies(far_chip, core, 5 * c, far_send.at[core])
    for copy in near_copies:
        copy.start()

    def wait_block(block):
        pltpu.make_async_copy(raw_s.at[block], raw_s.at[block], in_recv.at[block, 0]).wait()
        pltpu.make_async_copy(raw_m.at[block], raw_m.at[block], in_recv.at[block, 1]).wait()
        pltpu.make_async_copy(raw_w.at[block], raw_w.at[block], in_recv.at[block, 2]).wait()

    first = k == 0
    last = k == chips - 1
    lane = lax.broadcasted_iota(jnp.int32, (1, LANES), 1)

    def absent(block):
        if block < 2:
            return first
        if block > 3:
            return last
        return None

    def prepare(blocks, base, rows):
        count = 4 * len(blocks)
        for e in range(18):
            for n, block in enumerate(blocks):
                value = (raw_s if e < 9 else raw_m)[block, e % 9]
                gone = absent(block)
                if gone is not None:
                    value = jnp.where(gone, 1.0 if e == 4 else 0.0, value)
                lhs[e * count + 4 * n:e * count + 4 * n + 4, :] = value
        moved = permuted(lhs[0:18 * count, :], perm[...], 0)
        for e in range(18):
            for m in range(CHUNK):
                value = moved[e * count:(e + 1) * count, m * LANES:(m + 1) * LANES]
                if m == 0 and e % 3 == 0:
                    value = jnp.where(lane == 0, 0.0, value)
                if m == CHUNK - 1 and e % 3 == 2:
                    value = jnp.where(lane == LANES - 1, 0.0, value)
                ce[e * CHUNK + m, base:base + count, :] = value
        for n, block in enumerate(blocks):
            value = raw_w[block].reshape(64, 512)
            gone = absent(block)
            if gone is not None:
                value = jnp.where(gone, 0.0, value)
            value = permuted(value, perm[...], 0)
            for r in range(4):
                for half in range(2):
                    for m in range(CHUNK):
                        pb[0, rows[n] + r, m, half] = value[16 * r + 8 * half:16 * r + 8 * half + 8, m * LANES:(m + 1) * LANES]

    def factor_rows(s, lo, hi):
        def entry(e, m):
            return ce[e * CHUNK + m, lo:hi, :] + s * ce[(9 + e) * CHUNK + m, lo:hi, :]
        parts = line_factors(*[[entry(e, m) for m in range(CHUNK)] for e in (3, 4, 5)])
        for name, value in parts.items():
            fc[SLOT[name], lo:hi, :] = value
        for n, e in enumerate(OFF):
            for m in range(CHUNK):
                fc[len(NAMES) + n * CHUNK + m, lo:hi, :] = entry(e, m)

    def slot_of(r):
        return jnp.where(r < 4, r + 16, jnp.where(r < 20, r - 4, r))

    def spread(ref, index, slot):
        return ref[index, pl.ds(slot, 1), :][None]

    def line_group(it, r0, count=4):
        rows = [r0 + n for n in range(count)]
        slots = [slot_of(r) for r in rows]

        def co(name, n):
            return spread(fc, SLOT[name], slots[n])

        g, d = [], []
        for n, r in enumerate(rows):
            d0, d1, d2, d3 = [pb[it, r, m] for m in range(CHUNK)]
            d1 = d1 - co("w1", n) * d0
            d2 = d2 - co("w2", n) * d1
            g2 = d2 * co("i2", n)
            g1 = (d1 - co("c1", n) * g2) * co("i1", n)
            g0 = (d0 - co("c0", n) * g1) * co("i0", n)
            d.append(d3 - co("a3", n) * g2 - co("c3", n) * lane_roll(g0, -1))
            g.append((g0, g1, g2))
        for level in range(7):
            step = 1 << level
            d = [v + co("al%d" % level, n) * lane_roll(v, step) + co("ga%d" % level, n) * lane_roll(v, -step)
                 for n, v in enumerate(d)]
        for n, r in enumerate(rows):
            x3 = d[n] * co("inv", n)
            before = lane_roll(x3, 1)
            x0 = g[n][0] - co("e0", n) * before - co("f0", n) * x3
            x1 = g[n][1] - co("e1", n) * before - co("f1", n) * x3
            x2 = g[n][2] - co("e2", n) * before - co("f2", n) * x3
            zb[it, r, 0] = before
            zb[it, r, 1] = x0
            zb[it, r, 2] = x1
            zb[it, r, 3] = x2
            zb[it, r, 4] = x3
            zb[it, r, 5] = lane_roll(x0, -1)

    def off_row(it, r):
        slot = slot_of(r)
        for m in range(CHUNK):
            total = None
            for n, e in enumerate(OFF):
                source = zb[it, r + (-1 if e < 3 else 1), m + e % 3]
                term = spread(fc, len(NAMES) + n * CHUNK + m, slot) * source
                total = term if total is None else total + term
            pb[it + 1, r, m] = total

    def send_halo(do):
        for n, (chip, at) in enumerate(((down, 8), (up, 12))):
            copy = pltpu.make_async_remote_copy(
                src_ref=pb.at[0, pl.ds(at, 4)], dst_ref=hx.at[n], send_sem=hx_send.at[n], recv_sem=hx_recv.at[n],
                device_id=device(chip, c), device_id_type=MESH)
            do(copy)

    def ar_copy(t, n):
        return pltpu.make_async_remote_copy(
            src_ref=msg.at[t], dst_ref=arb.at[t, k], send_sem=ar_send.at[t], recv_sem=ar_recv.at[t],
            device_id=device(lax.rem(k + n, chips), c), device_id_type=MESH)

    def out_copies(n, dst_local, dst_remote):
        return (
            pltpu.make_async_copy(os_.at[n, pl.ds(4 * c, 4)], dst_local, out_local.at[n]),
            pltpu.make_async_remote_copy(
                src_ref=os_.at[n, pl.ds(4 - 4 * c, 4)], dst_ref=dst_remote, send_sem=out_send.at[n], recv_sem=out_recv.at[n],
                device_id=device(k, 1 - c), device_id_type=MESH),
        )

    half_cols = pl.ds(pl.multiple_of(16 * c, 16), 16)

    def out_ref(n):
        return low_hbm.at[n, :, half_cols, :]

    def native(source):
        flat = jnp.concatenate([source[:, m].reshape(128, LANES) for m in range(CHUNK)], axis=1)
        return permuted(flat, perm[...], 1).reshape(8, 16, 512)

    def emit_low(n):
        os_[n] = native(us[...])
        for copy in out_copies(n, out_ref(n), out_ref(n)):
            copy.start()

    for block in (2, 3, 1, 4):
        wait_block(block)
    for copy in far_copies:
        copy.start()
    prepare((1, 2, 3, 4), 0, (4, 8, 12, 16))

    lane8 = lax.broadcasted_iota(jnp.int32, (8, LANES), 1)

    def adi(t, carry):
        s = shifts[t]

        @pl.when(t == 1)
        def _():
            send_halo(lambda copy: copy.start())

        factor_rows(s, 0, 16)

        def main(it, carry):
            def groups(n, carry):
                line_group(it, jnp.minimum(4 + it + 4 * n, 16 - it))
                return carry
            lax.fori_loop(0, 4 - it // 2, groups, 0)

            def rows(n, carry):
                off_row(it, 5 + it + 2 * n)
                off_row(it, 6 + it + 2 * n)
                return carry
            lax.fori_loop(0, 7 - it, rows, 0)
            return carry
        lax.fori_loop(0, ITERS, main, 0)

        def dots(r, sums):
            sums = list(sums)
            for m in range(CHUNK):
                v = [pb[i, r, m] for i in range(ITERS + 1)]
                sums = [old + v[i] * v[j] for old, (i, j) in zip(sums, PAIRS)]
            return tuple(sums)
        sums = lax.fori_loop(8, 16, dots, tuple(jnp.zeros((2, 8, LANES), F32) for _ in PAIRS))
        packed = jnp.zeros((8, LANES), F32)
        for n, value in enumerate(sums):
            value = jnp.sum(value, axis=2, keepdims=True)
            for half in range(2):
                packed = jnp.where(lane8 == 16 * half + n, value[half], packed)
        msg[t] = packed
        arb[t, k] = packed

        def send(n, carry):
            ar_copy(t, n).start()
            return carry
        lax.fori_loop(1, chips, send, 0)

        @pl.when(t == 0)
        def _():
            wait_block(0)
            wait_block(5)
            prepare((0, 5), 16, (0, 20))

        @pl.when(t > 0)
        def _():
            emit_low(t - 1)

        @pl.when(t == 1)
        def _():
            send_halo(lambda copy: copy.wait())
            for n, at in enumerate((0, 20)):
                gone = first if n == 0 else last
                for r in range(4):
                    pb[0, at + r] = jnp.where(gone, 0.0, hx[n, r])

        @pl.when(t < 2)
        def _():
            factor_rows(s, 16, 24)

            def outer(it, carry):
                def side(n, carry):
                    line_group(it, jnp.where(n == 0, it, 20 - it))
                    return carry
                lax.fori_loop(0, 2, side, 0)

                @pl.when(it < ITERS - 1)
                def _():
                    def rows(n, carry):
                        off_row(it, it + 1 + n)
                        off_row(it, 19 - it + n)
                        return carry
                    lax.fori_loop(0, 4, rows, 0)
                return carry
            lax.fori_loop(0, ITERS, outer, 0)

        pltpu.make_async_copy(arb.at[t, pl.ds(0, chips - 1)], arb.at[t, pl.ds(0, chips - 1)], ar_recv.at[t]).wait()
        total = jnp.sum(arb[t], axis=0)
        gram = {}
        for n, pair in enumerate(PAIRS):
            gram[pair] = jnp.stack([
                jnp.broadcast_to(jnp.sum(jnp.where(lane8 == 16 * half + n, total, 0.0), axis=1, keepdims=True), (8, LANES))
                for half in range(2)])
        y = solve_weights(gram)
        scale = jnp.sqrt(jnp.full((1, 8, LANES), 2.0 * s, F32))

        def combine(r, carry):
            for m in range(6):
                total = y[0] * zb[0, r, m]
                for it in range(1, ITERS):
                    total = total + y[it] * zb[it, r, m]
                ub[r, m] = total
            return carry
        lax.fori_loop(jnp.where(t < 2, 3, 7), jnp.where(t < 2, 21, 17), combine, 0)

        def keep(r, carry):
            for m in range(CHUNK):
                us[r, m] = scale * ub[8 + r, 1 + m]
            return carry
        lax.fori_loop(0, 8, keep, 0)

        twice = 2.0 * s

        def update(r, carry):
            slot = slot_of(r)
            for m in range(CHUNK):
                total = None
                for e in range(9):
                    term = spread(ce, (9 + e) * CHUNK + m, slot) * ub[r + e // 3 - 1, m + e % 3]
                    total = term if total is None else total + term
                pb[0, r, m] = pb[0, r, m] - twice * total
            return carry
        lax.fori_loop(jnp.where(t < 2, 4, 8), jnp.where(t < 2, 20, 16), update, 0)
        return carry

    lax.fori_loop(0, STEPS, adi, 0)

    emit_low(STEPS - 1)
    os_[STEPS] = native(pb[0, 8:16])
    res_at = res_hbm.at[:, half_cols, :]
    for copy in out_copies(STEPS, res_at, res_at):
        copy.start()

    for copy in near_copies + far_copies:
        copy.wait_send()

    def drain(t, carry):
        pltpu.make_async_copy(arb.at[t, pl.ds(0, chips - 1)], arb.at[t, pl.ds(0, chips - 1)], ar_send.at[t]).wait()
        for copy in out_copies(t, out_ref(t), out_ref(t)):
            copy.wait()
        return carry
    lax.fori_loop(0, STEPS, drain, 0)
    for copy in out_copies(STEPS, res_at, res_at):
        copy.wait()


def solution(mesh):
    chips = mesh.shape["rows"] // 2

    def shards(stiffness, mass, shifts, factor):
        field = (24, CHUNK, 2, 8, LANES)
        framed = (24, CHUNK + 2, 2, 8, LANES)
        dma = pltpu.SemaphoreType.DMA
        return pl.pallas_call(
            functools.partial(kernel, chips),
            out_shape=(jax.ShapeDtypeStruct((STEPS, 4, 32, 512), F32), jax.ShapeDtypeStruct((4, 32, 512), F32)),
            in_specs=[pl.BlockSpec(memory_space=pltpu.SMEM)] + [pl.BlockSpec(memory_space=pl.ANY)] * 3,
            out_specs=(pl.BlockSpec(memory_space=pl.ANY), pl.BlockSpec(memory_space=pl.ANY)),
            scratch_shapes=[
                pltpu.VMEM((512, 512), BF16),
                pltpu.VMEM((6, 9, 4, 512), F32),
                pltpu.VMEM((6, 9, 4, 512), F32),
                pltpu.VMEM((6, 4, 16, 512), F32),
                pltpu.VMEM((18 * 16, 512), F32),
                pltpu.VMEM((18 * CHUNK, 24, LANES), F32),
                pltpu.VMEM((len(NAMES) + 6 * CHUNK, 24, LANES), F32),
                pltpu.VMEM((ITERS + 1,) + field, F32),
                pltpu.VMEM((ITERS,) + framed, F32),
                pltpu.VMEM(framed, F32),
                pltpu.VMEM((8, CHUNK, 2, 8, LANES), F32),
                pltpu.VMEM((STEPS + 1, 8, 16, 512), F32),
                pltpu.VMEM((STEPS, chips, 8, LANES), F32),
                pltpu.VMEM((2, 4, CHUNK, 2, 8, LANES), F32),
                pltpu.VMEM((STEPS, 8, LANES), F32),
                dma((3, 3)),
                dma((6, 3)),
                dma((2, 3)),
                dma((STEPS,)),
                dma((STEPS,)),
                dma((2,)),
                dma((2,)),
                dma((STEPS + 1,)),
                dma((STEPS + 1,)),
                dma((STEPS + 1,)),
            ],
            compiler_params=pltpu.CompilerParams(
                collective_id=0, has_side_effects=True, vmem_limit_bytes=48 << 20),
        )(shifts, stiffness, mass, factor)

    return jax.shard_map(
        shards,
        mesh=mesh,
        in_specs=(P(None, "rows", None), P(None, "rows", None), P(), P("rows", None, None)),
        out_specs=(P(None, "rows", None, None), P("rows", None, None)),
        check_vma=False,
    )
```

profile of v0, /device:TPU:1, one launch (start us, length us, event | category | flops | bytes accessed | tf_op | source)
XLA Modules:
  0.0 96.2 jit_solution(2458312156967668229)
XLA Ops:
  0.6 0.0 copy-start
  0.6 0.9 copy-done
  1.6 0.0 copy-start.1
  1.6 0.9 copy-done.1
  2.5 0.0 copy-start.2
  2.5 0.9 copy-done.2
  3.4 0.0 copy-start.3
  3.4 0.7 copy-done.3
  4.0 90.6 %shard_map.59 = (f32[3,4,32,512]{3,2,1,0:T(8,128)S(1)}, f32[4,32,512]{2,1,0:T(8,128)S(1)}) custom-call(f32[3]{0:T(128)S(1)} %copy-done.3, f32[9,4,512]{2,1,0:T(4,128)S(1)} %copy-done.1, f32[9,4,512]{2,1,0:T(4,128)S(1)} %copy-done.2, f32[4,32,512]{2,1,0:T(8,128)S(1)} %copy-done), custom_call_target="tpu_custom_call" | custom-call | tf_op jit(solution)/shard_map/pallas_call | solution.py:485
  94.6 0.9 copy.8
  95.5 0.7 copy.9
Async XLA Ops:
  0.6 1.0 copy-start
  1.6 0.9 copy-start.1
  2.5 0.9 copy-start.2
  3.4 0.7 copy-start.3
where the time goes:
time: 96.4 us; the launch traced here: 96.2 us
  Pallas kernels  90.6 us (94%)
  local copies, waits for them, and re-layouts  4.95 us (5%)
    pallas_call x1, Pallas kernels, shards(): pl.pallas_call(functools.partial(kernel, chips), out_shape=(jax.ShapeDtyp...  90.6 us
    unnamed x10, local copies, waits for them, and re-layouts  4.95 us

commit v1 on v0

v1 whole, which is shorter than its diff:
```python
import functools

import jax
import jax.numpy as jnp
from jax import lax
from jax.experimental import pallas as pl
from jax.experimental.pallas import tpu as pltpu
from jax.sharding import PartitionSpec as P

STEPS = 3
ITERS = 4
MESH = pl.DeviceIdType.MESH
PAIRS = [(i, j) for i in range(ITERS + 1) for j in range(i, ITERS + 1)]
LANES = 128
CHUNK = 8
HALF = 64
F32 = jnp.float32
BF16 = jnp.bfloat16

NAMES = ["w%d" % n for n in range(1, 7)] + ["i%d" % n for n in range(7)] + ["u%d" % n for n in range(6)]
NAMES += ["e%d" % n for n in range(7)] + ["f%d" % n for n in range(7)] + ["a7", "c7", "inv"]
NAMES += ["p%d%s%d" % (level, way, reach) for level in range(3) for way in "du" for reach in (1, 2, 3)]
SLOT = {name: n for n, name in enumerate(NAMES)}
OFF = (0, 1, 2, 6, 7, 8)
COUNT = len(NAMES) + len(OFF) * CHUNK


def lane_roll(x, shift):
    return pltpu.roll(x, shift % LANES, axis=x.ndim - 1)


def split3(x):
    a = x.astype(BF16)
    rest = x - a.astype(F32)
    b = rest.astype(BF16)
    c = (rest - b.astype(F32)).astype(BF16)
    return a, b, c


def permuted(x, perm, dim=0):
    total = None
    for part in split3(x):
        term = lax.dot_general(part, perm, (((1,), (dim,)), ((), ())), preferred_element_type=F32)
        total = term if total is None else total + term
    return total


def line_factors(a, b, c):
    out = {}
    last = CHUNK - 1
    i, u, w = [], [], [None]
    for m in range(last):
        pivot = b[m]
        if m:
            w.append(a[m] * i[m - 1])
            pivot = pivot - w[m] * c[m - 1]
        i.append(1.0 / pivot)
        u.append(c[m] * i[m])
    t = [a[0]]
    for m in range(1, last):
        t.append(-w[m] * t[m - 1])
    e, f = [None] * last, [None] * last
    e[last - 1] = t[last - 1] * i[last - 1]
    f[last - 1] = u[last - 1]
    for m in reversed(range(last - 1)):
        e[m] = t[m] * i[m] - u[m] * e[m + 1]
        f[m] = -u[m] * f[m + 1]
    for m in range(last):
        out["i%d" % m], out["e%d" % m], out["f%d" % m] = i[m], e[m], f[m]
        if m:
            out["w%d" % m] = w[m]
        if m < last - 1:
            out["u%d" % m] = u[m]
    out["a7"], out["c7"] = a[last], c[last]
    low = -a[last] * e[last - 1]
    mid = b[last] - a[last] * f[last - 1] - c[last] * lane_roll(e[0], -1)
    high = -c[last] * lane_roll(f[0], -1)
    for level in range(3):
        k = 1 << (2 * level)
        pairs = []
        for reach in (k, 2 * k):
            inv = 1.0 / mid
            al = -low * lane_roll(inv, reach)
            ga = -high * lane_roll(inv, -reach)
            mid = mid + al * lane_roll(high, reach) + ga * lane_roll(low, -reach)
            low, high = al * lane_roll(low, reach), ga * lane_roll(high, -reach)
            pairs.append((al, ga))
        (al1, ga1), (al2, ga2) = pairs
        merged = {
            "d1": al1 + al2 * lane_roll(ga1, 2 * k), "d2": al2, "d3": al2 * lane_roll(al1, 2 * k),
            "u1": ga1 + ga2 * lane_roll(al1, -2 * k), "u2": ga2, "u3": ga2 * lane_roll(ga1, -2 * k),
        }
        for key, value in merged.items():
            out["p%d%s" % (level, key)] = value
    inv = 1.0 / mid
    out["inv"] = inv
    for key in ("d1", "d2", "d3", "u1", "u2", "u3"):
        out["p2" + key] = out["p2" + key] * inv
    return out


def least_squares(columns, initial):
    count = len(columns)
    cosines, sines = [], []
    rhs = [initial] + [None] * count
    upper = []
    for position in range(count):
        column = list(columns[position])
        for earlier in range(position):
            first = cosines[earlier] * column[earlier] + sines[earlier] * column[earlier + 1]
            second = -sines[earlier] * column[earlier] + cosines[earlier] * column[earlier + 1]
            column[earlier], column[earlier + 1] = first, second
        radius = jnp.sqrt(column[position] * column[position] + column[position + 1] * column[position + 1])
        inverse = 1.0 / radius
        cosine = column[position] * inverse
        sine = column[position + 1] * inverse
        cosines.append(cosine)
        sines.append(sine)
        rhs[position + 1] = -sine * rhs[position]
        rhs[position] = cosine * rhs[position]
        upper.append(column[:position] + [inverse])
    y = [None] * count
    for position in reversed(range(count)):
        accum = rhs[position]
        for onward in range(position + 1, count):
            accum = accum - upper[onward][position] * y[onward]
        y[position] = accum * upper[position][position]
    return y


def solve_weights(gram):
    n = ITERS + 1
    r = {}
    for i in range(n):
        pivot = gram[(i, i)]
        for m in range(i):
            pivot = pivot - r[(m, i)] * r[(m, i)]
        pivot = jnp.maximum(pivot, gram[(i, i)] * 1e-9)
        root = jnp.sqrt(pivot)
        r[(i, i)] = root
        inverse = 1.0 / root
        for j in range(i + 1, n):
            value = gram[(i, j)]
            for m in range(i):
                value = value - r[(m, i)] * r[(m, j)]
            r[(i, j)] = value * inverse
    columns = []
    for k in range(ITERS):
        columns.append([r[(i, k)] + r[(i, k + 1)] for i in range(k + 1)] + [r[(k + 1, k + 1)]])
    return least_squares(columns, r[(0, 0)])


def kernel(chips, shifts, stiff_hbm, mass_hbm, factor_hbm, low_hbm, res_hbm,
           perm, own_s, own_m, own_w, lhs, send_c, send_w, raw_c, ce, fc, pb, zb, ub, us, os_, arb, hx, msg,
           own_sem, in_send, in_recv, far_send, ar_send, ar_recv, hx_send, hx_recv, out_send, out_recv, out_local):
    me = lax.axis_index("rows")
    k = me // 2
    c = me % 2
    up = lax.rem(k + chips - 1, chips)
    down = lax.rem(k + 1, chips)

    def device(chip, core):
        return (chip * 2 + core,)

    barrier = pltpu.get_barrier_semaphore()

    def greet(n, carry):
        pl.semaphore_signal(barrier, inc=1, device_id=device(lax.rem(k + n, chips), c), device_id_type=MESH)
        return carry

    for chip in (k, up, down):
        pl.semaphore_signal(barrier, inc=1, device_id=device(chip, 1 - c), device_id_type=MESH)
    lax.fori_loop(1, chips, greet, 0)

    own_copies = [
        pltpu.make_async_copy(stiff_hbm, own_s, own_sem.at[0]),
        pltpu.make_async_copy(mass_hbm, own_m, own_sem.at[1]),
        pltpu.make_async_copy(factor_hbm, own_w, own_sem.at[2]),
    ]
    for copy in own_copies:
        copy.start()

    row = lax.broadcasted_iota(jnp.int32, (512, CHUNK * LANES), 0)
    col = lax.broadcasted_iota(jnp.int32, (512, CHUNK * LANES), 1)
    perm[...] = jnp.where(row == CHUNK * (col % HALF) + col // LANES, 1.0, 0.0).astype(BF16)

    lane = lax.broadcasted_iota(jnp.int32, (8, LANES), 1)
    left = lane < HALF
    lane1 = lax.broadcasted_iota(jnp.int32, (1, LANES), 1)
    left1 = lane1 < HALF
    first = k == 0
    last = k == chips - 1
    own = 2 + c

    for copy in own_copies:
        copy.wait()
    for e in range(18):
        lhs[4 * e:4 * e + 4, :] = own_s[e] if e < 9 else own_m[e - 9]
    moved = permuted(lhs[0:72, :], perm[...])
    for q in range(4):
        send_c[:, q * LANES:(q + 1) * LANES] = jnp.where(
            left1, moved[:, 2 * q * LANES:(2 * q + 1) * LANES], moved[:, (2 * q + 1) * LANES:(2 * q + 2) * LANES])
    moved = permuted(own_w[...].reshape(128, 512), perm[...])
    for core in range(2):
        for r in range(4):
            at = 32 * r + 16 * core
            for m in range(CHUNK):
                span = slice(m * LANES, (m + 1) * LANES)
                send_w[core, r, m] = jnp.where(left, moved[at:at + 8, span], moved[at + 8:at + 16, span])
    raw_c[own] = send_c[...]
    pb[0, pl.ds(4 * own, 4)] = send_w[c]

    pl.semaphore_wait(barrier, chips - 1 + 3)

    def block_copies(chip, core, block, sems):
        return [
            pltpu.make_async_remote_copy(
                src_ref=send_c, dst_ref=raw_c.at[block],
                send_sem=sems.at[0], recv_sem=in_recv.at[block, 0], device_id=device(chip, core), device_id_type=MESH),
            pltpu.make_async_remote_copy(
                src_ref=send_w.at[core], dst_ref=pb.at[0, pl.ds(4 * block, 4)],
                send_sem=sems.at[1], recv_sem=in_recv.at[block, 1], device_id=device(chip, core), device_id_type=MESH),
        ]

    near_chip = lax.rem(k + 2 * c - 1 + chips, chips)
    far_chip = lax.rem(k + 1 - 2 * c + chips, chips)
    near_copies = []
    for core in range(2):
        near_copies += block_copies(near_chip, core, 4 - 3 * c, in_send.at[core])
    near_copies += block_copies(k, 1 - c, own, in_send.at[2])
    far_copies = []
    for core in range(2):
        far_copies += block_copies(far_chip, core, 5 * c, far_send.at[core])
    for copy in near_copies:
        copy.start()

    def wait_block(block):
        pltpu.make_async_copy(raw_c.at[block], raw_c.at[block], in_recv.at[block, 0]).wait()
        rows = pb.at[0, pl.ds(4 * block, 4)]
        pltpu.make_async_copy(rows, rows, in_recv.at[block, 1]).wait()

    def absent(block):
        if block < 2:
            return first
        if block > 3:
            return last
        return None

    def prepare(blocks, base):
        count = 4 * len(blocks)
        for e in range(18):
            for n, block in enumerate(blocks):
                value = raw_c[block, 4 * e:4 * e + 4, :]
                gone = absent(block)
                if gone is not None:
                    value = jnp.where(gone, 1.0 if e == 4 else 0.0, value)
                lhs[e * count + 4 * n:e * count + 4 * n + 4, :] = value
        for e in range(18):
            for q in range(4):
                value = lhs[e * count:(e + 1) * count, q * LANES:(q + 1) * LANES]
                other = lane_roll(value, HALF)
                both = [jnp.where(left1, value, other), jnp.where(left1, other, value)]
                if q == 0 and e % 3 == 0:
                    both[0] = jnp.where(lane1 % HALF == 0, 0.0, both[0])
                if q == 3 and e % 3 == 2:
                    both[1] = jnp.where(lane1 % HALF == HALF - 1, 0.0, both[1])
                for n in range(2):
                    ce[e * CHUNK + 2 * q + n, base:base + count, :] = both[n]
        for block in blocks:
            gone = absent(block)
            if gone is not None:
                @pl.when(gone)
                def _():
                    pb[0, 4 * block:4 * block + 4] = jnp.zeros((4, CHUNK, 8, LANES), F32)

    def factor_rows(t, lo, hi):
        s = shifts[t]
        par = lax.rem(t, 2)

        def entry(e, m):
            return ce[e * CHUNK + m, lo:hi, :] + s * ce[(9 + e) * CHUNK + m, lo:hi, :]
        parts = line_factors(*[[entry(e, m) for m in range(CHUNK)] for e in (3, 4, 5)])
        for name, value in parts.items():
            fc[par, SLOT[name], lo:hi, :] = value
        for n, e in enumerate(OFF):
            for m in range(CHUNK):
                fc[par, len(NAMES) + n * CHUNK + m, lo:hi, :] = entry(e, m)

    def slot_of(r):
        return jnp.where(r < 4, r + 16, jnp.where(r < 20, r - 4, r))

    def line_group(par, it, rows):
        slots = [slot_of(r) for r in rows]

        def co(name, n):
            return fc[par, SLOT[name], pl.ds(slots[n], 1), :]

        g, d = [], []
        for n, r in enumerate(rows):
            v = [pb[it, r, m] for m in range(CHUNK)]
            for m in range(1, CHUNK - 1):
                v[m] = v[m] - co("w%d" % m, n) * v[m - 1]
            x = [v[m] * co("i%d" % m, n) for m in range(CHUNK - 1)]
            for m in reversed(range(CHUNK - 2)):
                x[m] = x[m] - co("u%d" % m, n) * x[m + 1]
            d.append(v[-1] - co("a7", n) * x[-1] - co("c7", n) * lane_roll(x[0], -1))
            g.append(x)
        for level in range(3):
            step = 1 << (2 * level)
            new = []
            for n, v in enumerate(d):
                total = v if level < 2 else v * co("inv", n)
                for reach in (1, 2, 3):
                    total = total + (co("p%dd%d" % (level, reach), n) * lane_roll(v, reach * step)
                                     + co("p%du%d" % (level, reach), n) * lane_roll(v, -reach * step))
                new.append(total)
            d = new
        for n, r in enumerate(rows):
            after = d[n]
            before = lane_roll(after, 1)
            zb[it, r, 0] = before
            zb[it, r, CHUNK] = after
            for m in range(CHUNK - 1):
                value = g[n][m] - co("e%d" % m, n) * before - co("f%d" % m, n) * after
                zb[it, r, m + 1] = value
                if m == 0:
                    zb[it, r, CHUNK + 1] = lane_roll(value, -1)

    def off_row(par, it, r):
        slot = slot_of(r)
        for m in range(CHUNK):
            total = None
            for n, e in enumerate(OFF):
                source = zb[it, r + (-1 if e < 3 else 1), m + e % 3]
                term = fc[par, len(NAMES) + n * CHUNK + m, pl.ds(slot, 1), :] * source
                total = term if total is None else total + term
            pb[it + 1, r, m] = total

    def send_halo(do):
        for n, (chip, at) in enumerate(((down, 8), (up, 12))):
            copy = pltpu.make_async_remote_copy(
                src_ref=pb.at[0, pl.ds(at, 4)], dst_ref=hx.at[n], send_sem=hx_send.at[n], recv_sem=hx_recv.at[n],
                device_id=device(chip, c), device_id_type=MESH)
            do(copy)

    def ar_copy(t, n):
        return pltpu.make_async_remote_copy(
            src_ref=msg.at[t], dst_ref=arb.at[t, k], send_sem=ar_send.at[t], recv_sem=ar_recv.at[t],
            device_id=device(lax.rem(k + n, chips), c), device_id_type=MESH)

    def out_copies(n, dst):
        return (
            pltpu.make_async_copy(os_.at[n, pl.ds(4 * c, 4)], dst, out_local.at[n]),
            pltpu.make_async_remote_copy(
                src_ref=os_.at[n, pl.ds(4 - 4 * c, 4)], dst_ref=dst, send_sem=out_send.at[n], recv_sem=out_recv.at[n],
                device_id=device(k, 1 - c), device_id_type=MESH),
        )

    half_cols = pl.ds(pl.multiple_of(16 * c, 16), 16)

    def out_ref(n):
        return low_hbm.at[n, :, half_cols, :]

    def native(source):
        flat = jnp.concatenate([source[:, m].reshape(64, LANES) for m in range(CHUNK)], axis=1)
        whole = lax.broadcasted_iota(jnp.int32, (64, CHUNK * LANES), 1) % LANES < HALF
        halves = [permuted(jnp.where(whole, flat, 0.0), perm[...], 1), permuted(jnp.where(whole, 0.0, flat), perm[...], 1)]
        return [half.reshape(8, 8, 512) for half in halves]

    def emit(n, source, dst):
        halves = native(source)
        for h in range(2):
            os_[n, :, 8 * h:8 * h + 8, :] = halves[h]
        for copy in out_copies(n, dst):
            copy.start()

    for block in (2, 3):
        @pl.when(block == 3 - c)
        def _():
            wait_block(block)
    wait_block(1)
    wait_block(4)
    for copy in far_copies:
        copy.start()
    prepare((1, 2, 3, 4), 0)
    factor_rows(0, 0, 16)

    def adi(t, carry):
        s = shifts[t]
        par = lax.rem(t, 2)

        @pl.when(t == 1)
        def _():
            send_halo(lambda copy: copy.start())

        def main(it, carry):
            line_group(par, it, [4 + n for n in range(16)])

            def rows(n, carry):
                off_row(par, it, 5 + it + 2 * n)
                off_row(par, it, 6 + it + 2 * n)
                return carry
            lax.fori_loop(0, 7 - it, rows, 0)
            return carry
        lax.fori_loop(0, ITERS, main, 0)

        def dots(r, sums):
            sums = list(sums)
            for m in range(CHUNK):
                v = [pb[i, r, m] for i in range(ITERS + 1)]
                sums = [old + v[i] * v[j] for old, (i, j) in zip(sums, PAIRS)]
            return tuple(sums)
        sums = lax.fori_loop(8, 16, dots, tuple(jnp.zeros((8, LANES), F32) for _ in PAIRS))
        packed = jnp.zeros((8, LANES), F32)
        for n, value in enumerate(sums):
            for half in range(2):
                part = jnp.sum(jnp.where(left, value, 0.0) if half == 0 else jnp.where(left, 0.0, value), axis=1, keepdims=True)
                packed = jnp.where(lane == 16 * half + n, part, packed)
        msg[t] = packed
        arb[t, k] = packed

        def send(n, carry):
            ar_copy(t, n).start()
            return carry
        lax.fori_loop(1, chips, send, 0)

        @pl.when(t == 0)
        def _():
            wait_block(0)
            wait_block(5)
            prepare((0, 5), 16)
            factor_rows(t, 16, 24)

        @pl.when(t == 1)
        def _():
            send_halo(lambda copy: copy.wait())
            for n, at in enumerate((0, 20)):
                gone = first if n == 0 else last
                for r in range(4):
                    pb[0, at + r] = jnp.where(gone, 0.0, hx[n, r])

        @pl.when(t < 2)
        def _():
            def outer(it, carry):
                line_group(par, it, [it + n for n in range(4)] + [20 - it + n for n in range(4)])

                @pl.when(it < ITERS - 1)
                def _():
                    def rows(n, carry):
                        off_row(par, it, it + 1 + n)
                        off_row(par, it, 19 - it + n)
                        return carry
                    lax.fori_loop(0, 4, rows, 0)
                return carry
            lax.fori_loop(0, ITERS, outer, 0)
            factor_rows(t + 1, 0, 24)

        @pl.when(t > 0)
        def _():
            emit(t - 1, us[...], out_ref(t - 1))

        pltpu.make_async_copy(arb.at[t, pl.ds(0, chips - 1)], arb.at[t, pl.ds(0, chips - 1)], ar_recv.at[t]).wait()
        total = jnp.sum(arb[t], axis=0)
        gram = {}
        for n, pair in enumerate(PAIRS):
            part = [jnp.sum(jnp.where(lane == 16 * half + n, total, 0.0), axis=1, keepdims=True) for half in range(2)]
            gram[pair] = jnp.where(left, part[0], part[1])
        y = solve_weights(gram)
        scale = jnp.sqrt(jnp.full((8, LANES), 2.0 * s, F32))

        def combine(r, carry):
            for m in range(CHUNK + 2):
                total = y[0] * zb[0, r, m]
                for it in range(1, ITERS):
                    total = total + y[it] * zb[it, r, m]
                ub[r, m] = total
            return carry
        lax.fori_loop(jnp.where(t < 2, 3, 7), jnp.where(t < 2, 21, 17), combine, 0)

        def keep(r, carry):
            for m in range(CHUNK):
                us[r, m] = scale * ub[8 + r, 1 + m]
            return carry
        lax.fori_loop(0, 8, keep, 0)

        twice = 2.0 * s

        def update(r, carry):
            slot = slot_of(r)
            for m in range(CHUNK):
                total = None
                for e in range(9):
                    term = ce[(9 + e) * CHUNK + m, pl.ds(slot, 1), :] * ub[r + e // 3 - 1, m + e % 3]
                    total = term if total is None else total + term
                pb[0, r, m] = pb[0, r, m] - twice * total
            return carry
        lax.fori_loop(jnp.where(t < 2, 4, 8), jnp.where(t < 2, 20, 16), update, 0)
        return carry

    lax.fori_loop(0, STEPS, adi, 0)

    res_at = res_hbm.at[:, half_cols, :]
    emit(STEPS - 1, us[...], out_ref(STEPS - 1))
    emit(STEPS, pb[0, 8:16], res_at)

    for copy in near_copies + far_copies:
        copy.wait_send()

    def drain(t, carry):
        pltpu.make_async_copy(arb.at[t, pl.ds(0, chips - 1)], arb.at[t, pl.ds(0, chips - 1)], ar_send.at[t]).wait()
        for copy in out_copies(t, out_ref(t)):
            copy.wait()
        return carry
    lax.fori_loop(0, STEPS, drain, 0)
    for copy in out_copies(STEPS, res_at):
        copy.wait()


def solution(mesh):
    chips = mesh.shape["rows"] // 2

    def shards(stiffness, mass, shifts, factor):
        field = (24, CHUNK, 8, LANES)
        framed = (24, CHUNK + 2, 8, LANES)
        dma = pltpu.SemaphoreType.DMA
        return pl.pallas_call(
            functools.partial(kernel, chips),
            out_shape=(jax.ShapeDtypeStruct((STEPS, 4, 32, 512), F32), jax.ShapeDtypeStruct((4, 32, 512), F32)),
            in_specs=[pl.BlockSpec(memory_space=pltpu.SMEM)] + [pl.BlockSpec(memory_space=pl.ANY)] * 3,
            out_specs=(pl.BlockSpec(memory_space=pl.ANY), pl.BlockSpec(memory_space=pl.ANY)),
            scratch_shapes=[
                pltpu.VMEM((512, CHUNK * LANES), BF16),
                pltpu.VMEM((9, 4, 512), F32),
                pltpu.VMEM((9, 4, 512), F32),
                pltpu.VMEM((4, 32, 512), F32),
                pltpu.VMEM((18 * 16, 512), F32),
                pltpu.VMEM((18 * 4, 512), F32),
                pltpu.VMEM((2, 4, CHUNK, 8, LANES), F32),
                pltpu.VMEM((6, 18 * 4, 512), F32),
                pltpu.VMEM((18 * CHUNK, 24, LANES), F32),
                pltpu.VMEM((2, COUNT, 24, LANES), F32),
                pltpu.VMEM((ITERS + 1,) + field, F32),
                pltpu.VMEM((ITERS,) + framed, F32),
                pltpu.VMEM(framed, F32),
                pltpu.VMEM((8, CHUNK, 8, LANES), F32),
                pltpu.VMEM((STEPS + 1, 8, 16, 512), F32),
                pltpu.VMEM((STEPS, chips, 8, LANES), F32),
                pltpu.VMEM((2, 4, CHUNK, 8, LANES), F32),
                pltpu.VMEM((STEPS, 8, LANES), F32),
                dma((3,)),
                dma((3, 2)),
                dma((6, 2)),
                dma((2, 2)),
                dma((STEPS,)),
                dma((STEPS,)),
                dma((2,)),
                dma((2,)),
                dma((STEPS + 1,)),
                dma((STEPS + 1,)),
                dma((STEPS + 1,)),
            ],
            compiler_params=pltpu.CompilerParams(
                collective_id=0, has_side_effects=True, vmem_limit_bytes=60 << 20),
        )(shifts, stiffness, mass, factor)

    return jax.shard_map(
        shards,
        mesh=mesh,
        in_specs=(P(None, "rows", None), P(None, "rows", None), P(), P("rows", None, None)),
        out_specs=(P(None, "rows", None, None), P("rows", None, None)),
        check_vma=False,
    )
```

time: 96.4 us -> 70.8 us (0.73)
  Pallas kernels: 90.6 us -> 67.2 us
  local copies, waits for them, and re-layouts: 4.95 us -> 2.81 us
    pallas_call x1, Pallas kernels: 90.6 us -> 67.2 us  [shards(): pl.pallas_call(functools.partial(kernel, chips), out_shape=(jax.ShapeDtyp...]
    unnamed x10 -> x4, local copies, waits for them, and re-layouts: 4.95 us -> 2.81 us
where the time goes in v1:
time: 70.8 us; the launch traced here: 70.7 us
  Pallas kernels  67.2 us (95%)
  local copies, waits for them, and re-layouts  2.81 us (4%)
    pallas_call x1, Pallas kernels, shards(): pl.pallas_call(functools.partial(kernel, chips), out_shape=(jax.ShapeDtyp...  67.2 us
    unnamed x4, local copies, waits for them, and re-layouts  2.81 us

profile of v1, /device:TPU:1, one launch (start us, length us, event | category | flops | bytes accessed | tf_op | source)
XLA Modules:
  0.0 70.7 jit_solution(16630449468170903527)
XLA Ops:
  0.6 67.2 %shard_map.59 = (f32[3,4,32,512]{3,2,1,0:T(8,128)}, f32[4,32,512]{2,1,0:T(8,128)}) custom-call(f32[3]{0:T(128)} %shifts.1, f32[9,4,512]{2,1,0:T(4,128)} %stiff_hbm.1, f32[9,4,512]{2,1,0:T(4,128)} %mass_hbm.1, f32[4,32,512]{2,1,0:T(8,128)} %factor_hbm.1), custom_call_target="tpu_custom_call" | custom-call | tf_op jit(solution)/shard_map/pallas_call | solution.py:526
  67.9 0.0 copy-start
  67.9 2.1 %copy.8 = f32[3,4,32,512]{3,2,1,0:T(8,128)} copy(f32[3,4,32,512]{3,2,1,0:T(8,128)} %get-tuple-element.4) | data formatting | bytes 1572864
  70.0 0.0 copy-done
  70.0 0.7 copy.9
Async XLA Ops:
  67.9 2.1 %copy-start = (f32[4,32,512]{2,1,0:T(8,128)S(1)}, f32[4,32,512]{2,1,0:T(8,128)}, u32[]{:S(2)}) copy-start(f32[4,32,512]{2,1,0:T(8,128)} %get-tuple-element.5) | copy-start | bytes 786436

commit v2 on v1

--- a/solution.py
+++ b/solution.py
@@ -38,11 +38,9 @@
 
 
 def permuted(x, perm, dim=0):
-    total = None
-    for part in split3(x):
-        term = lax.dot_general(part, perm, (((1,), (dim,)), ((), ())), preferred_element_type=F32)
-        total = term if total is None else total + term
-    return total
+    rows = x.shape[0]
+    moved = lax.dot_general(jnp.concatenate(split3(x), axis=0), perm, (((1,), (dim,)), ((), ())), preferred_element_type=F32)
+    return moved[:rows] + moved[rows:2 * rows] + moved[2 * rows:]
 
 
 def line_factors(a, b, c):
@@ -151,7 +149,7 @@
 
 
 def kernel(chips, shifts, stiff_hbm, mass_hbm, factor_hbm, low_hbm, res_hbm,
-           perm, own_s, own_m, own_w, lhs, send_c, send_w, raw_c, ce, fc, pb, zb, ub, us, os_, arb, hx, msg,
+           perm, own_s, own_m, own_w, lhs, send_c, send_w, raw_c, ce, fc, pb, zb, ub, os_, arb, hx, msg,
            own_sem, in_send, in_recv, far_send, ar_send, ar_recv, hx_send, hx_recv, out_send, out_recv, out_local):
     me = lax.axis_index("rows")
     k = me // 2
@@ -180,9 +178,9 @@
     for copy in own_copies:
         copy.start()
 
-    row = lax.broadcasted_iota(jnp.int32, (512, CHUNK * LANES), 0)
-    col = lax.broadcasted_iota(jnp.int32, (512, CHUNK * LANES), 1)
-    perm[...] = jnp.where(row == CHUNK * (col % HALF) + col // LANES, 1.0, 0.0).astype(BF16)
+    row = lax.broadcasted_iota(jnp.int32, (512, 512), 0)
+    col = lax.broadcasted_iota(jnp.int32, (512, 512), 1)
+    perm[...] = jnp.where(row == CHUNK * (col % HALF) + col // HALF, 1.0, 0.0).astype(BF16)
 
     lane = lax.broadcasted_iota(jnp.int32, (8, LANES), 1)
     left = lane < HALF
@@ -196,17 +194,16 @@
         copy.wait()
     for e in range(18):
         lhs[4 * e:4 * e + 4, :] = own_s[e] if e < 9 else own_m[e - 9]
-    moved = permuted(lhs[0:72, :], perm[...])
-    for q in range(4):
-        send_c[:, q * LANES:(q + 1) * LANES] = jnp.where(
-            left1, moved[:, 2 * q * LANES:(2 * q + 1) * LANES], moved[:, (2 * q + 1) * LANES:(2 * q + 2) * LANES])
+    send_c[...] = permuted(lhs[0:72, :], perm[...])
     moved = permuted(own_w[...].reshape(128, 512), perm[...])
     for core in range(2):
         for r in range(4):
             at = 32 * r + 16 * core
-            for m in range(CHUNK):
-                span = slice(m * LANES, (m + 1) * LANES)
-                send_w[core, r, m] = jnp.where(left, moved[at:at + 8, span], moved[at + 8:at + 16, span])
+            for q in range(4):
+                one = moved[at:at + 8, q * LANES:(q + 1) * LANES]
+                two = moved[at + 8:at + 16, q * LANES:(q + 1) * LANES]
+                send_w[core, r, 2 * q] = jnp.where(left, one, lane_roll(two, HALF))
+                send_w[core, r, 2 * q + 1] = jnp.where(left, lane_roll(one, HALF), two)
     raw_c[own] = send_c[...]
     pb[0, pl.ds(4 * own, 4)] = send_w[c]
 
@@ -336,6 +333,15 @@
                 total = term if total is None else total + term
             pb[it + 1, r, m] = total
 
+    if chips == 64:
+        ahead = [[lax.rem(lax.div(k, stride) + n, 4) * stride for n in range(4)] for stride in (16, 4, 1)]
+        spans = sorted(
+            ((a, b, d) for a in range(4) for b in range(4) for d in range(4) if (a, b, d) != (0, 0, 0)),
+            key=lambda offset: -sum(min(n, 4 - n) for n in offset))
+        others = [ahead[0][a] + ahead[1][b] + ahead[2][d] for a, b, d in spans]
+    else:
+        others = [lax.rem(k + n, chips) for n in range(1, chips)]
+
     def send_halo(do):
         for n, (chip, at) in enumerate(((down, 8), (up, 12))):
             copy = pltpu.make_async_remote_copy(
@@ -343,10 +349,10 @@
                 device_id=device(chip, c), device_id_type=MESH)
             do(copy)
 
-    def ar_copy(t, n):
+    def ar_copy(t, chip):
         return pltpu.make_async_remote_copy(
             src_ref=msg.at[t], dst_ref=arb.at[t, k], send_sem=ar_send.at[t], recv_sem=ar_recv.at[t],
-            device_id=device(lax.rem(k + n, chips), c), device_id_type=MESH)
+            device_id=device(chip, c), device_id_type=MESH)
 
     def out_copies(n, dst):
         return (
@@ -362,10 +368,14 @@
         return low_hbm.at[n, :, half_cols, :]
 
     def native(source):
-        flat = jnp.concatenate([source[:, m].reshape(64, LANES) for m in range(CHUNK)], axis=1)
-        whole = lax.broadcasted_iota(jnp.int32, (64, CHUNK * LANES), 1) % LANES < HALF
-        halves = [permuted(jnp.where(whole, flat, 0.0), perm[...], 1), permuted(jnp.where(whole, 0.0, flat), perm[...], 1)]
-        return [half.reshape(8, 8, 512) for half in halves]
+        whole = left[None]
+        tiles = [[], []]
+        for q in range(4):
+            even, odd = source[:, 2 * q], source[:, 2 * q + 1]
+            tiles[0].append(jnp.where(whole, even, lane_roll(odd, HALF)).reshape(64, LANES))
+            tiles[1].append(jnp.where(whole, lane_roll(even, HALF), odd).reshape(64, LANES))
+        flat = jnp.concatenate([jnp.concatenate(t, axis=1) for t in tiles], axis=0)
+        return permuted(flat, perm[...], 1).reshape(2, 8, 8, 512)
 
     def emit(n, source, dst):
         halves = native(source)
@@ -374,24 +384,26 @@
         for copy in out_copies(n, dst):
             copy.start()
 
+    def emit_low(n):
+        scale = jnp.sqrt(jnp.full((1, 1, 8, LANES), 2.0 * shifts[n], F32))
+        emit(n, scale * ub[8:16, 1:CHUNK + 1], out_ref(n))
+
     for block in (2, 3):
         @pl.when(block == 3 - c)
         def _():
             wait_block(block)
+    for copy in near_copies:
+        copy.wait_send()
+    for copy in far_copies:
+        copy.start()
     wait_block(1)
     wait_block(4)
-    for copy in far_copies:
-        copy.start()
     prepare((1, 2, 3, 4), 0)
     factor_rows(0, 0, 16)
 
     def adi(t, carry):
         s = shifts[t]
         par = lax.rem(t, 2)
-
-        @pl.when(t == 1)
-        def _():
-            send_halo(lambda copy: copy.start())
 
         def main(it, carry):
             line_group(par, it, [4 + n for n in range(16)])
@@ -419,17 +431,24 @@
         msg[t] = packed
         arb[t, k] = packed
 
-        def send(n, carry):
-            ar_copy(t, n).start()
-            return carry
-        lax.fori_loop(1, chips, send, 0)
+        for chip in others:
+            ar_copy(t, chip).start()
+
+        @pl.when(t < 2)
+        def _():
+            factor_rows(t + 1, 0, 16)
+
+        @pl.when(t > 0)
+        def _():
+            emit_low(t - 1)
 
         @pl.when(t == 0)
         def _():
             wait_block(0)
             wait_block(5)
             prepare((0, 5), 16)
-            factor_rows(t, 16, 24)
+            factor_rows(0, 16, 24)
+            factor_rows(1, 16, 24)
 
         @pl.when(t == 1)
         def _():
@@ -453,11 +472,6 @@
                     lax.fori_loop(0, 4, rows, 0)
                 return carry
             lax.fori_loop(0, ITERS, outer, 0)
-            factor_rows(t + 1, 0, 24)
-
-        @pl.when(t > 0)
-        def _():
-            emit(t - 1, us[...], out_ref(t - 1))
 
         pltpu.make_async_copy(arb.at[t, pl.ds(0, chips - 1)], arb.at[t, pl.ds(0, chips - 1)], ar_recv.at[t]).wait()
         total = jnp.sum(arb[t], axis=0)
@@ -466,7 +480,6 @@
             part = [jnp.sum(jnp.where(lane == 16 * half + n, total, 0.0), axis=1, keepdims=True) for half in range(2)]
             gram[pair] = jnp.where(left, part[0], part[1])
         y = solve_weights(gram)
-        scale = jnp.sqrt(jnp.full((8, LANES), 2.0 * s, F32))
 
         def combine(r, carry):
             for m in range(CHUNK + 2):
@@ -475,13 +488,6 @@
                     total = total + y[it] * zb[it, r, m]
                 ub[r, m] = total
             return carry
-        lax.fori_loop(jnp.where(t < 2, 3, 7), jnp.where(t < 2, 21, 17), combine, 0)
-
-        def keep(r, carry):
-            for m in range(CHUNK):
-                us[r, m] = scale * ub[8 + r, 1 + m]
-            return carry
-        lax.fori_loop(0, 8, keep, 0)
 
         twice = 2.0 * s
 
@@ -494,16 +500,28 @@
                     total = term if total is None else total + term
                 pb[0, r, m] = pb[0, r, m] - twice * total
             return carry
-        lax.fori_loop(jnp.where(t < 2, 4, 8), jnp.where(t < 2, 20, 16), update, 0)
+        lax.fori_loop(7, 17, combine, 0)
+        lax.fori_loop(8, 16, update, 0)
+
+        @pl.when(t == 0)
+        def _():
+            send_halo(lambda copy: copy.start())
+
+        @pl.when(t < 2)
+        def _():
+            lax.fori_loop(3, 7, combine, 0)
+            lax.fori_loop(17, 21, combine, 0)
+            lax.fori_loop(4, 8, update, 0)
+            lax.fori_loop(16, 20, update, 0)
         return carry
 
     lax.fori_loop(0, STEPS, adi, 0)
 
     res_at = res_hbm.at[:, half_cols, :]
-    emit(STEPS - 1, us[...], out_ref(STEPS - 1))
+    emit_low(STEPS - 1)
     emit(STEPS, pb[0, 8:16], res_at)
 
-    for copy in near_copies + far_copies:
+    for copy in far_copies:
         copy.wait_send()
 
     def drain(t, carry):
@@ -529,7 +547,7 @@
             in_specs=[pl.BlockSpec(memory_space=pltpu.SMEM)] + [pl.BlockSpec(memory_space=pl.ANY)] * 3,
             out_specs=(pl.BlockSpec(memory_space=pl.ANY), pl.BlockSpec(memory_space=pl.ANY)),
             scratch_shapes=[
-                pltpu.VMEM((512, CHUNK * LANES), BF16),
+                pltpu.VMEM((512, 512), BF16),
                 pltpu.VMEM((9, 4, 512), F32),
                 pltpu.VMEM((9, 4, 512), F32),
                 pltpu.VMEM((4, 32, 512), F32),
@@ -542,7 +560,6 @@
                 pltpu.VMEM((ITERS + 1,) + field, F32),
                 pltpu.VMEM((ITERS,) + framed, F32),
                 pltpu.VMEM(framed, F32),
-                pltpu.VMEM((8, CHUNK, 8, LANES), F32),
                 pltpu.VMEM((STEPS + 1, 8, 16, 512), F32),
                 pltpu.VMEM((STEPS, chips, 8, LANES), F32),
                 pltpu.VMEM((2, 4, CHUNK, 8, LANES), F32),

time: 70.8 us -> 61.3 us (0.87)
  Pallas kernels: 67.2 us -> 57.7 us
    pallas_call x1, Pallas kernels: 67.2 us -> 57.7 us  [shards(): pl.pallas_call(functools.partial(kernel, chips), out_shape=(jax.ShapeDtyp...]
where the time goes in v2:
time: 61.3 us; the launch traced here: 61.2 us
  Pallas kernels  57.7 us (94%)
  local copies, waits for them, and re-layouts  2.81 us (5%)
  between operations  0.65 us (1%)
    pallas_call x1, Pallas kernels, shards(): pl.pallas_call(functools.partial(kernel, chips), out_shape=(jax.ShapeDtyp...  57.7 us
    unnamed x4, local copies, waits for them, and re-layouts  2.81 us

profile of v2, /device:TPU:1, one launch (start us, length us, event | category | flops | bytes accessed | tf_op | source)
XLA Modules:
  0.0 61.2 jit_solution(2797345236844568073)
XLA Ops:
  0.6 57.7 %shard_map.59 = (f32[3,4,32,512]{3,2,1,0:T(8,128)}, f32[4,32,512]{2,1,0:T(8,128)}) custom-call(f32[3]{0:T(128)} %shifts.1, f32[9,4,512]{2,1,0:T(4,128)} %stiff_hbm.1, f32[9,4,512]{2,1,0:T(4,128)} %mass_hbm.1, f32[4,32,512]{2,1,0:T(8,128)} %factor_hbm.1), custom_call_target="tpu_custom_call" | custom-call | tf_op jit(solution)/shard_map/pallas_call | solution.py:544
  58.4 0.0 copy-start
  58.4 2.1 %copy.8 = f32[3,4,32,512]{3,2,1,0:T(8,128)} copy(f32[3,4,32,512]{3,2,1,0:T(8,128)} %get-tuple-element.4) | data formatting | bytes 1572864
  60.5 0.0 copy-done
  60.5 0.7 %copy.9 = f32[4,32,512]{2,1,0:T(8,128)} copy(f32[4,32,512]{2,1,0:T(8,128)S(1)} %copy-done) | data formatting | bytes 524288
Async XLA Ops:
  58.4 2.1 %copy-start = (f32[4,32,512]{2,1,0:T(8,128)S(1)}, f32[4,32,512]{2,1,0:T(8,128)}, u32[]{:S(2)}) copy-start(f32[4,32,512]{2,1,0:T(8,128)} %get-tuple-element.5) | copy-start | bytes 786436

commit v3 on v2

--- a/solution.py
+++ b/solution.py
@@ -18,7 +18,7 @@
 BF16 = jnp.bfloat16
 
 NAMES = ["w%d" % n for n in range(1, 7)] + ["i%d" % n for n in range(7)] + ["u%d" % n for n in range(6)]
-NAMES += ["e%d" % n for n in range(7)] + ["f%d" % n for n in range(7)] + ["a7", "c7", "inv"]
+NAMES += ["e%d" % n for n in range(7)] + ["f%d" % n for n in range(7)] + ["a7", "c7", "inv", "en", "fn"]
 NAMES += ["p%d%s%d" % (level, way, reach) for level in range(3) for way in "du" for reach in (1, 2, 3)]
 SLOT = {name: n for n, name in enumerate(NAMES)}
 OFF = (0, 1, 2, 6, 7, 8)
@@ -70,9 +70,10 @@
         if m < last - 1:
             out["u%d" % m] = u[m]
     out["a7"], out["c7"] = a[last], c[last]
+    out["en"], out["fn"] = lane_roll(e[0], -1), lane_roll(f[0], -1)
     low = -a[last] * e[last - 1]
-    mid = b[last] - a[last] * f[last - 1] - c[last] * lane_roll(e[0], -1)
-    high = -c[last] * lane_roll(f[0], -1)
+    mid = b[last] - a[last] * f[last - 1] - c[last] * out["en"]
+    high = -c[last] * out["fn"]
     for level in range(3):
         k = 1 << (2 * level)
         pairs = []
@@ -148,8 +149,8 @@
     return least_squares(columns, r[(0, 0)])
 
 
-def kernel(chips, shifts, stiff_hbm, mass_hbm, factor_hbm, low_hbm, res_hbm,
-           perm, own_s, own_m, own_w, lhs, send_c, send_w, raw_c, ce, fc, pb, zb, ub, os_, arb, hx, msg,
+def kernel(chips, shifts_hbm, stiff_hbm, mass_hbm, factor_hbm, low_hbm, res_hbm,
+           perm, own_s, own_m, own_w, lhs, send_c, send_w, raw_c, ce, fc, pb, zb, ub, os_, arb, hx, msg, shifts,
            own_sem, in_send, in_recv, far_send, ar_send, ar_recv, hx_send, hx_recv, out_send, out_recv, out_local):
     me = lax.axis_index("rows")
     k = me // 2
@@ -162,18 +163,25 @@
 
     barrier = pltpu.get_barrier_semaphore()
 
-    def greet(n, carry):
-        pl.semaphore_signal(barrier, inc=1, device_id=device(lax.rem(k + n, chips), c), device_id_type=MESH)
-        return carry
-
-    for chip in (k, up, down):
+    if chips == 64:
+        ahead = [[lax.rem(lax.div(k, stride) + n, 4) * stride for n in range(4)] for stride in (16, 4, 1)]
+        spans = sorted(
+            ((a, b, d) for a in range(4) for b in range(4) for d in range(4) if (a, b, d) != (0, 0, 0)),
+            key=lambda offset: -sum(min(n, 4 - n) for n in offset))
+        others = [ahead[0][a] + ahead[1][b] + ahead[2][d] for a, b, d in spans]
+    else:
+        others = [lax.rem(k + n, chips) for n in range(1, chips)]
+
+    for chip in (up, down, k):
         pl.semaphore_signal(barrier, inc=1, device_id=device(chip, 1 - c), device_id_type=MESH)
-    lax.fori_loop(1, chips, greet, 0)
+    for chip in others:
+        pl.semaphore_signal(barrier, inc=1, device_id=device(chip, c), device_id_type=MESH)
 
     own_copies = [
         pltpu.make_async_copy(stiff_hbm, own_s, own_sem.at[0]),
         pltpu.make_async_copy(mass_hbm, own_m, own_sem.at[1]),
         pltpu.make_async_copy(factor_hbm, own_w, own_sem.at[2]),
+        pltpu.make_async_copy(shifts_hbm, shifts, own_sem.at[3]),
     ]
     for copy in own_copies:
         copy.start()
@@ -184,6 +192,11 @@
 
     lane = lax.broadcasted_iota(jnp.int32, (8, LANES), 1)
     left = lane < HALF
+    sub = lax.broadcasted_iota(jnp.int32, (8, LANES), 0)
+    halves8 = jnp.where((sub % 2 == 0) == left, 1.0, 0.0).astype(BF16)
+    sub16 = lax.broadcasted_iota(jnp.int32, (16, LANES), 0)
+    lane16 = lax.broadcasted_iota(jnp.int32, (16, LANES), 1)
+    halves16 = jnp.where(sub16 == lane16 // HALF, 1.0, 0.0).astype(BF16)
     lane1 = lax.broadcasted_iota(jnp.int32, (1, LANES), 1)
     left1 = lane1 < HALF
     first = k == 0
@@ -221,18 +234,19 @@
 
     near_chip = lax.rem(k + 2 * c - 1 + chips, chips)
     far_chip = lax.rem(k + 1 - 2 * c + chips, chips)
-    near_copies = []
+    near_copies, far_copies = [], []
     for core in range(2):
-        near_copies += block_copies(near_chip, core, 4 - 3 * c, in_send.at[core])
-    near_copies += block_copies(k, 1 - c, own, in_send.at[2])
-    far_copies = []
-    for core in range(2):
+        near_copies.append(block_copies(near_chip, core, 4 - 3 * c, in_send.at[core]))
         far_copies += block_copies(far_chip, core, 5 * c, far_send.at[core])
+    near_copies.append(block_copies(k, 1 - c, own, in_send.at[2]))
+    near_copies = [pair[0] for pair in near_copies] + [pair[1] for pair in near_copies]
     for copy in near_copies:
         copy.start()
 
-    def wait_block(block):
+    def wait_stencil(block):
         pltpu.make_async_copy(raw_c.at[block], raw_c.at[block], in_recv.at[block, 0]).wait()
+
+    def wait_field(block):
         rows = pb.at[0, pl.ds(4 * block, 4)]
         pltpu.make_async_copy(rows, rows, in_recv.at[block, 1]).wait()
 
@@ -263,12 +277,11 @@
                     both[1] = jnp.where(lane1 % HALF == HALF - 1, 0.0, both[1])
                 for n in range(2):
                     ce[e * CHUNK + 2 * q + n, base:base + count, :] = both[n]
-        for block in blocks:
-            gone = absent(block)
-            if gone is not None:
-                @pl.when(gone)
-                def _():
-                    pb[0, 4 * block:4 * block + 4] = jnp.zeros((4, CHUNK, 8, LANES), F32)
+
+    def clear(block):
+        @pl.when(absent(block))
+        def _():
+            pb[0, 4 * block:4 * block + 4] = jnp.zeros((4, CHUNK, 8, LANES), F32)
 
     def factor_rows(t, lo, hi):
         s = shifts[t]
@@ -292,7 +305,7 @@
         def co(name, n):
             return fc[par, SLOT[name], pl.ds(slots[n], 1), :]
 
-        g, d = [], []
+        g, d, ahead_g = [], [], []
         for n, r in enumerate(rows):
             v = [pb[it, r, m] for m in range(CHUNK)]
             for m in range(1, CHUNK - 1):
@@ -300,7 +313,8 @@
             x = [v[m] * co("i%d" % m, n) for m in range(CHUNK - 1)]
             for m in reversed(range(CHUNK - 2)):
                 x[m] = x[m] - co("u%d" % m, n) * x[m + 1]
-            d.append(v[-1] - co("a7", n) * x[-1] - co("c7", n) * lane_roll(x[0], -1))
+            ahead_g.append(lane_roll(x[0], -1))
+            d.append(v[-1] - co("a7", n) * x[-1] - co("c7", n) * ahead_g[-1])
             g.append(x)
         for level in range(3):
             step = 1 << (2 * level)
@@ -318,10 +332,8 @@
             zb[it, r, 0] = before
             zb[it, r, CHUNK] = after
             for m in range(CHUNK - 1):
-                value = g[n][m] - co("e%d" % m, n) * before - co("f%d" % m, n) * after
-                zb[it, r, m + 1] = value
-                if m == 0:
-                    zb[it, r, CHUNK + 1] = lane_roll(value, -1)
+                zb[it, r, m + 1] = g[n][m] - co("e%d" % m, n) * before - co("f%d" % m, n) * after
+            zb[it, r, CHUNK + 1] = ahead_g[n] - co("en", n) * after - co("fn", n) * lane_roll(after, -1)
 
     def off_row(par, it, r):
         slot = slot_of(r)
@@ -333,15 +345,6 @@
                 total = term if total is None else total + term
             pb[it + 1, r, m] = total
 
-    if chips == 64:
-        ahead = [[lax.rem(lax.div(k, stride) + n, 4) * stride for n in range(4)] for stride in (16, 4, 1)]
-        spans = sorted(
-            ((a, b, d) for a in range(4) for b in range(4) for d in range(4) if (a, b, d) != (0, 0, 0)),
-            key=lambda offset: -sum(min(n, 4 - n) for n in offset))
-        others = [ahead[0][a] + ahead[1][b] + ahead[2][d] for a, b, d in spans]
-    else:
-        others = [lax.rem(k + n, chips) for n in range(1, chips)]
-
     def send_halo(do):
         for n, (chip, at) in enumerate(((down, 8), (up, 12))):
             copy = pltpu.make_async_remote_copy(
@@ -391,43 +394,49 @@
     for block in (2, 3):
         @pl.when(block == 3 - c)
         def _():
-            wait_block(block)
+            wait_stencil(block)
+    wait_stencil(1)
+    wait_stencil(4)
+    prepare((1, 2, 3, 4), 0)
+    factor_rows(0, 0, 16)
     for copy in near_copies:
         copy.wait_send()
     for copy in far_copies:
         copy.start()
-    wait_block(1)
-    wait_block(4)
-    prepare((1, 2, 3, 4), 0)
-    factor_rows(0, 0, 16)
+    for block in (2, 3):
+        @pl.when(block == 3 - c)
+        def _():
+            wait_field(block)
+    for block in (1, 4):
+        wait_field(block)
+        clear(block)
 
     def adi(t, carry):
         s = shifts[t]
         par = lax.rem(t, 2)
 
-        def main(it, carry):
-            line_group(par, it, [4 + n for n in range(16)])
+        sums = {pair: jnp.zeros((8, LANES), F32) for pair in PAIRS}
+
+        def dots(latest):
+            for r in range(8, 16):
+                for m in range(CHUNK):
+                    newest = pb[latest, r, m]
+                    for i in range(latest + 1):
+                        sums[(i, latest)] = sums[(i, latest)] + newest * (newest if i == latest else pb[i, r, m])
+
+        for it in range(ITERS):
+            line_group(par, it, list(range(4 + it, 20 - it)))
+            dots(it)
 
             def rows(n, carry):
                 off_row(par, it, 5 + it + 2 * n)
                 off_row(par, it, 6 + it + 2 * n)
                 return carry
             lax.fori_loop(0, 7 - it, rows, 0)
-            return carry
-        lax.fori_loop(0, ITERS, main, 0)
-
-        def dots(r, sums):
-            sums = list(sums)
-            for m in range(CHUNK):
-                v = [pb[i, r, m] for i in range(ITERS + 1)]
-                sums = [old + v[i] * v[j] for old, (i, j) in zip(sums, PAIRS)]
-            return tuple(sums)
-        sums = lax.fori_loop(8, 16, dots, tuple(jnp.zeros((8, LANES), F32) for _ in PAIRS))
-        packed = jnp.zeros((8, LANES), F32)
-        for n, value in enumerate(sums):
-            for half in range(2):
-                part = jnp.sum(jnp.where(left, value, 0.0) if half == 0 else jnp.where(left, 0.0, value), axis=1, keepdims=True)
-                packed = jnp.where(lane == 16 * half + n, part, packed)
+        dots(ITERS)
+        stacked = jnp.concatenate([sums[pair] for pair in PAIRS] + [jnp.zeros((8, LANES), F32)], axis=0)
+        packed = lax.dot_general(halves16, jnp.concatenate(split3(stacked), axis=0), (((1,), (1,)), ((), ())), preferred_element_type=F32)
+        packed = packed[0:2, 0:LANES] + packed[0:2, LANES:2 * LANES] + packed[0:2, 2 * LANES:]
         msg[t] = packed
         arb[t, k] = packed
 
@@ -444,11 +453,14 @@
 
         @pl.when(t == 0)
         def _():
-            wait_block(0)
-            wait_block(5)
+            for block in (0, 5):
+                wait_stencil(block)
             prepare((0, 5), 16)
             factor_rows(0, 16, 24)
             factor_rows(1, 16, 24)
+            for block in (0, 5):
+                wait_field(block)
+                clear(block)
 
         @pl.when(t == 1)
         def _():
@@ -475,10 +487,11 @@
 
         pltpu.make_async_copy(arb.at[t, pl.ds(0, chips - 1)], arb.at[t, pl.ds(0, chips - 1)], ar_recv.at[t]).wait()
         total = jnp.sum(arb[t], axis=0)
-        gram = {}
-        for n, pair in enumerate(PAIRS):
-            part = [jnp.sum(jnp.where(lane == 16 * half + n, total, 0.0), axis=1, keepdims=True) for half in range(2)]
-            gram[pair] = jnp.where(left, part[0], part[1])
+        total = jnp.concatenate([total] * 3 + [jnp.zeros((2, LANES), F32)], axis=0)
+        one, two, three = [part.astype(F32) for part in split3(total)]
+        total = jnp.where(sub < 2, one, jnp.where(sub < 4, two, three)).astype(BF16)
+        spread_out = lax.dot_general(total, halves8, (((0,), (0,)), ((), ())), preferred_element_type=F32)
+        gram = {pair: spread_out[8 * n:8 * n + 8] for n, pair in enumerate(PAIRS)}
         y = solve_weights(gram)
 
         def combine(r, carry):
@@ -500,8 +513,8 @@
                     total = term if total is None else total + term
                 pb[0, r, m] = pb[0, r, m] - twice * total
             return carry
-        lax.fori_loop(7, 17, combine, 0)
-        lax.fori_loop(8, 16, update, 0)
+        lax.fori_loop(7, 17, combine, 0, unroll=2)
+        lax.fori_loop(8, 16, update, 0, unroll=2)
 
         @pl.when(t == 0)
         def _():
@@ -511,8 +524,8 @@
         def _():
             lax.fori_loop(3, 7, combine, 0)
             lax.fori_loop(17, 21, combine, 0)
-            lax.fori_loop(4, 8, update, 0)
-            lax.fori_loop(16, 20, update, 0)
+            lax.fori_loop(4, 8, update, 0, unroll=2)
+            lax.fori_loop(16, 20, update, 0, unroll=2)
         return carry
 
     lax.fori_loop(0, STEPS, adi, 0)
@@ -544,7 +557,7 @@
         return pl.pallas_call(
             functools.partial(kernel, chips),
             out_shape=(jax.ShapeDtypeStruct((STEPS, 4, 32, 512), F32), jax.ShapeDtypeStruct((4, 32, 512), F32)),
-            in_specs=[pl.BlockSpec(memory_space=pltpu.SMEM)] + [pl.BlockSpec(memory_space=pl.ANY)] * 3,
+            in_specs=[pl.BlockSpec(memory_space=pl.ANY)] * 4,
             out_specs=(pl.BlockSpec(memory_space=pl.ANY), pl.BlockSpec(memory_space=pl.ANY)),
             scratch_shapes=[
                 pltpu.VMEM((512, 512), BF16),
@@ -561,10 +574,11 @@
                 pltpu.VMEM((ITERS,) + framed, F32),
                 pltpu.VMEM(framed, F32),
                 pltpu.VMEM((STEPS + 1, 8, 16, 512), F32),
-                pltpu.VMEM((STEPS, chips, 8, LANES), F32),
+                pltpu.VMEM((STEPS, chips, 2, LANES), F32),
                 pltpu.VMEM((2, 4, CHUNK, 8, LANES), F32),
-                pltpu.VMEM((STEPS, 8, LANES), F32),
-                dma((3,)),
+                pltpu.VMEM((STEPS, 2, LANES), F32),
+                pltpu.SMEM((STEPS,), F32),
+                dma((4,)),
                 dma((3, 2)),
                 dma((6, 2)),
                 dma((2, 2)),

time: 61.3 us -> 57.5 us (0.938)
  Pallas kernels: 57.7 us -> 53.9 us
    pallas_call x1, Pallas kernels: 57.7 us -> 53.9 us  [shards(): pl.pallas_call(functools.partial(kernel, chips), out_shape=(jax.ShapeDtyp...]
where the time goes in v3:
time: 57.5 us; the launch traced here: 57.4 us
  Pallas kernels  53.9 us (94%)
  local copies, waits for them, and re-layouts  2.81 us (5%)
  between operations  0.65 us (1%)
    pallas_call x1, Pallas kernels, shards(): pl.pallas_call(functools.partial(kernel, chips), out_shape=(jax.ShapeDtyp...  53.9 us
    unnamed x4, local copies, waits for them, and re-layouts  2.81 us

profile of v3, /device:TPU:1, one launch (start us, length us, event | category | flops | bytes accessed | tf_op | source)
XLA Modules:
  0.0 57.4 jit_solution(17509233928140717399)
XLA Ops:
  0.6 53.9 %shard_map.59 = (f32[3,4,32,512]{3,2,1,0:T(8,128)}, f32[4,32,512]{2,1,0:T(8,128)}) custom-call(f32[3]{0:T(128)} %shifts_hbm.1, f32[9,4,512]{2,1,0:T(4,128)} %stiff_hbm.1, f32[9,4,512]{2,1,0:T(4,128)} %mass_hbm.1, f32[4,32,512]{2,1,0:T(8,128)} %factor_hbm.1), custom_call_target="tpu_custom_call" | custom-call | tf_op jit(solution)/shard_map/pallas_call | solution.py:557
  54.5 0.0 copy-start
  54.5 2.1 %copy.8 = f32[3,4,32,512]{3,2,1,0:T(8,128)} copy(f32[3,4,32,512]{3,2,1,0:T(8,128)} %get-tuple-element.4) | data formatting | bytes 1572864
  56.6 0.0 copy-done
  56.7 0.7 %copy.9 = f32[4,32,512]{2,1,0:T(8,128)} copy(f32[4,32,512]{2,1,0:T(8,128)S(1)} %copy-done) | data formatting | bytes 524288
Async XLA Ops:
  54.5 2.1 %copy-start = (f32[4,32,512]{2,1,0:T(8,128)S(1)}, f32[4,32,512]{2,1,0:T(8,128)}, u32[]{:S(2)}) copy-start(f32[4,32,512]{2,1,0:T(8,128)} %get-tuple-element.5) | copy-start | bytes 786436

commit v4 on v3

--- a/solution.py
+++ b/solution.py
@@ -150,8 +150,8 @@
 
 
 def kernel(chips, shifts_hbm, stiff_hbm, mass_hbm, factor_hbm, low_hbm, res_hbm,
-           perm, own_s, own_m, own_w, lhs, send_c, send_w, raw_c, ce, fc, pb, zb, ub, os_, arb, hx, msg, shifts,
-           own_sem, in_send, in_recv, far_send, ar_send, ar_recv, hx_send, hx_recv, out_send, out_recv, out_local):
+           perm, own_s, own_m, own_w, lhs, send_c, send_w, raw_c, ce, fc, pb, zb, ub, mz, os_, arb, hx, msg, shifts,
+           own_sem, hand_send, in_send, in_recv, far_send, ar_send, ar_recv, hx_send, hx_recv, out_send, out_recv, out_local):
     me = lax.axis_index("rows")
     k = me // 2
     c = me % 2
@@ -207,7 +207,9 @@
         copy.wait()
     for e in range(18):
         lhs[4 * e:4 * e + 4, :] = own_s[e] if e < 9 else own_m[e - 9]
-    send_c[...] = permuted(lhs[0:72, :], perm[...])
+    moved = permuted(lhs[0:72, :], perm[...])
+    for part in range(2):
+        send_c[part] = moved[36 * part:36 * part + 36]
     moved = permuted(own_w[...].reshape(128, 512), perm[...])
     for core in range(2):
         for r in range(4):
@@ -222,33 +224,46 @@
 
     pl.semaphore_wait(barrier, chips - 1 + 3)
 
-    def block_copies(chip, core, block, sems):
-        return [
-            pltpu.make_async_remote_copy(
-                src_ref=send_c, dst_ref=raw_c.at[block],
-                send_sem=sems.at[0], recv_sem=in_recv.at[block, 0], device_id=device(chip, core), device_id_type=MESH),
-            pltpu.make_async_remote_copy(
-                src_ref=send_w.at[core], dst_ref=pb.at[0, pl.ds(4 * block, 4)],
-                send_sem=sems.at[1], recv_sem=in_recv.at[block, 1], device_id=device(chip, core), device_id_type=MESH),
-        ]
+    def field_copy(chip, core, block, sem):
+        return pltpu.make_async_remote_copy(
+            src_ref=send_w.at[core], dst_ref=pb.at[0, pl.ds(4 * block, 4)],
+            send_sem=sem, recv_sem=in_recv.at[block, 2], device_id=device(chip, core), device_id_type=MESH)
+
+    def stencil_copy(chip, core, block, part, sem):
+        return pltpu.make_async_remote_copy(
+            src_ref=send_c.at[part], dst_ref=raw_c.at[block, part],
+            send_sem=sem, recv_sem=in_recv.at[block, part], device_id=device(chip, core), device_id_type=MESH)
+
+    def hand_on(block, n):
+        return pltpu.make_async_remote_copy(
+            src_ref=raw_c.at[block, c], dst_ref=raw_c.at[block, c],
+            send_sem=hand_send.at[n], recv_sem=in_recv.at[block, c], device_id=device(k, 1 - c), device_id_type=MESH)
 
     near_chip = lax.rem(k + 2 * c - 1 + chips, chips)
     far_chip = lax.rem(k + 1 - 2 * c + chips, chips)
-    near_copies, far_copies = [], []
-    for core in range(2):
-        near_copies.append(block_copies(near_chip, core, 4 - 3 * c, in_send.at[core]))
-        far_copies += block_copies(far_chip, core, 5 * c, far_send.at[core])
-    near_copies.append(block_copies(k, 1 - c, own, in_send.at[2]))
-    near_copies = [pair[0] for pair in near_copies] + [pair[1] for pair in near_copies]
+    near_copies = [stencil_copy(near_chip, core, 4 - 3 * c, core, in_send.at[core, 0]) for core in range(2)]
+    near_copies += [stencil_copy(k, 1 - c, own, part, in_send.at[2, part]) for part in range(2)]
+    near_copies += [field_copy(near_chip, core, 4 - 3 * c, in_send.at[core, 1]) for core in range(2)]
+    near_copies += [field_copy(k, 1 - c, own, in_send.at[2, 2])]
+    far_copies = [stencil_copy(far_chip, core, 5 * c, core, far_send.at[core, 0]) for core in range(2)]
+    far_copies += [field_copy(far_chip, core, 5 * c, far_send.at[core, 1]) for core in range(2)]
     for copy in near_copies:
         copy.start()
 
-    def wait_stencil(block):
-        pltpu.make_async_copy(raw_c.at[block], raw_c.at[block], in_recv.at[block, 0]).wait()
+    def wait_part(block, part):
+        half = raw_c.at[block, part]
+        pltpu.make_async_copy(half, half, in_recv.at[block, part]).wait()
 
     def wait_field(block):
         rows = pb.at[0, pl.ds(4 * block, 4)]
-        pltpu.make_async_copy(rows, rows, in_recv.at[block, 1]).wait()
+        pltpu.make_async_copy(rows, rows, in_recv.at[block, 2]).wait()
+
+    def wait_stencils(blocks):
+        for block in blocks:
+            wait_part(block, c)
+            hand_on(block, block).start()
+        for block in blocks:
+            wait_part(block, 1 - c)
 
     def absent(block):
         if block < 2:
@@ -261,7 +276,7 @@
         count = 4 * len(blocks)
         for e in range(18):
             for n, block in enumerate(blocks):
-                value = raw_c[block, 4 * e:4 * e + 4, :]
+                value = raw_c[block, e // 9, 4 * (e % 9):4 * (e % 9) + 4, :]
                 gone = absent(block)
                 if gone is not None:
                     value = jnp.where(gone, 1.0 if e == 4 else 0.0, value)
@@ -345,6 +360,14 @@
                 total = term if total is None else total + term
             pb[it + 1, r, m] = total
 
+    def mass_row(it, n):
+        for m in range(CHUNK):
+            total = None
+            for e in range(9):
+                term = ce[(9 + e) * CHUNK + m, pl.ds(n + 4, 1), :] * zb[it, n + 7 + e // 3, m + e % 3]
+                total = term if total is None else total + term
+            mz[it, n, m] = total
+
     def send_halo(do):
         for n, (chip, at) in enumerate(((down, 8), (up, 12))):
             copy = pltpu.make_async_remote_copy(
@@ -394,9 +417,9 @@
     for block in (2, 3):
         @pl.when(block == 3 - c)
         def _():
-            wait_stencil(block)
-    wait_stencil(1)
-    wait_stencil(4)
+            for part in range(2):
+                wait_part(block, part)
+    wait_stencils((1, 4))
     prepare((1, 2, 3, 4), 0)
     factor_rows(0, 0, 16)
     for copy in near_copies:
@@ -451,10 +474,17 @@
         def _():
             emit_low(t - 1)
 
+        def images(n, carry):
+            it = n // 4
+            r = 2 * (n % 4)
+            mass_row(it, r)
+            mass_row(it, r + 1)
+            return carry
+        lax.fori_loop(0, 4 * ITERS, images, 0)
+
         @pl.when(t == 0)
         def _():
-            for block in (0, 5):
-                wait_stencil(block)
+            wait_stencils((0, 5))
             prepare((0, 5), 16)
             factor_rows(0, 16, 24)
             factor_rows(1, 16, 24)
@@ -513,17 +543,27 @@
                     total = term if total is None else total + term
                 pb[0, r, m] = pb[0, r, m] - twice * total
             return carry
-        lax.fori_loop(7, 17, combine, 0, unroll=2)
-        lax.fori_loop(8, 16, update, 0, unroll=2)
+        scaled = [twice * value for value in y]
+
+        def update_own(n, carry):
+            for m in range(CHUNK):
+                total = scaled[0] * mz[0, n, m]
+                for it in range(1, ITERS):
+                    total = total + scaled[it] * mz[it, n, m]
+                pb[0, 8 + n, m] = pb[0, 8 + n, m] - total
+            return carry
+        lax.fori_loop(0, 8, update_own, 0, unroll=2)
 
         @pl.when(t == 0)
         def _():
             send_halo(lambda copy: copy.start())
 
+        lax.fori_loop(8, 16, combine, 0, unroll=2)
+
         @pl.when(t < 2)
         def _():
-            lax.fori_loop(3, 7, combine, 0)
-            lax.fori_loop(17, 21, combine, 0)
+            lax.fori_loop(3, 8, combine, 0)
+            lax.fori_loop(16, 21, combine, 0)
             lax.fori_loop(4, 8, update, 0, unroll=2)
             lax.fori_loop(16, 20, update, 0, unroll=2)
         return carry
@@ -536,6 +576,8 @@
 
     for copy in far_copies:
         copy.wait_send()
+    for block in (0, 1, 4, 5):
+        hand_on(block, block).wait_send()
 
     def drain(t, carry):
         pltpu.make_async_copy(arb.at[t, pl.ds(0, chips - 1)], arb.at[t, pl.ds(0, chips - 1)], ar_send.at[t]).wait()
@@ -565,22 +607,24 @@
                 pltpu.VMEM((9, 4, 512), F32),
                 pltpu.VMEM((4, 32, 512), F32),
                 pltpu.VMEM((18 * 16, 512), F32),
-                pltpu.VMEM((18 * 4, 512), F32),
+                pltpu.VMEM((2, 36, 512), F32),
                 pltpu.VMEM((2, 4, CHUNK, 8, LANES), F32),
-                pltpu.VMEM((6, 18 * 4, 512), F32),
+                pltpu.VMEM((6, 2, 36, 512), F32),
                 pltpu.VMEM((18 * CHUNK, 24, LANES), F32),
                 pltpu.VMEM((2, COUNT, 24, LANES), F32),
                 pltpu.VMEM((ITERS + 1,) + field, F32),
                 pltpu.VMEM((ITERS,) + framed, F32),
                 pltpu.VMEM(framed, F32),
+                pltpu.VMEM((ITERS, 8, CHUNK, 8, LANES), F32),
                 pltpu.VMEM((STEPS + 1, 8, 16, 512), F32),
                 pltpu.VMEM((STEPS, chips, 2, LANES), F32),
                 pltpu.VMEM((2, 4, CHUNK, 8, LANES), F32),
                 pltpu.VMEM((STEPS, 2, LANES), F32),
                 pltpu.SMEM((STEPS,), F32),
                 dma((4,)),
-                dma((3, 2)),
-                dma((6, 2)),
+                dma((6,)),
+                dma((3, 3)),
+                dma((6, 3)),
                 dma((2, 2)),
                 dma((STEPS,)),
                 dma((STEPS,)),

time: 57.5 us -> 57.9 us (level)
  no operation moved by 1% of the time
where the time goes in v4:
time: 57.9 us; the launch traced here: 57.7 us
  Pallas kernels  54.3 us (94%)
  local copies, waits for them, and re-layouts  2.81 us (5%)
  between operations  0.65 us (1%)
    pallas_call x1, Pallas kernels, shards(): pl.pallas_call(functools.partial(kernel, chips), out_shape=(jax.ShapeDtyp...  54.3 us
    unnamed x4, local copies, waits for them, and re-layouts  2.81 us

profile of v4, /device:TPU:1, one launch (start us, length us, event | category | flops | bytes accessed | tf_op | source)
XLA Modules:
  0.0 57.7 jit_solution(7649607170439693636)
XLA Ops:
  0.6 54.3 %shard_map.59 = (f32[3,4,32,512]{3,2,1,0:T(8,128)}, f32[4,32,512]{2,1,0:T(8,128)}) custom-call(f32[3]{0:T(128)} %shifts_hbm.1, f32[9,4,512]{2,1,0:T(4,128)} %stiff_hbm.1, f32[9,4,512]{2,1,0:T(4,128)} %mass_hbm.1, f32[4,32,512]{2,1,0:T(8,128)} %factor_hbm.1), custom_call_target="tpu_custom_call" | custom-call | tf_op jit(solution)/shard_map/pallas_call | solution.py:599
  54.9 0.0 copy-start
  54.9 2.1 %copy.8 = f32[3,4,32,512]{3,2,1,0:T(8,128)} copy(f32[3,4,32,512]{3,2,1,0:T(8,128)} %get-tuple-element.4) | data formatting | bytes 1572864
  57.0 0.0 copy-done
  57.0 0.7 %copy.9 = f32[4,32,512]{2,1,0:T(8,128)} copy(f32[4,32,512]{2,1,0:T(8,128)S(1)} %copy-done) | data formatting | bytes 524288
Async XLA Ops:
  54.9 2.1 %copy-start = (f32[4,32,512]{2,1,0:T(8,128)S(1)}, f32[4,32,512]{2,1,0:T(8,128)}, u32[]{:S(2)}) copy-start(f32[4,32,512]{2,1,0:T(8,128)} %get-tuple-element.5) | copy-start | bytes 786436

commit v5 on v3

--- a/solution.py
+++ b/solution.py
@@ -150,7 +150,7 @@
 
 
 def kernel(chips, shifts_hbm, stiff_hbm, mass_hbm, factor_hbm, low_hbm, res_hbm,
-           perm, own_s, own_m, own_w, lhs, send_c, send_w, raw_c, ce, fc, pb, zb, ub, os_, arb, hx, msg, shifts,
+           perm, own_s, own_m, own_w, lhs, send_c, send_w, raw_c, ce, fc, pb, zb, ub, mz, zn, os_, arb, hx, msg, shifts,
            own_sem, in_send, in_recv, far_send, ar_send, ar_recv, hx_send, hx_recv, out_send, out_recv, out_local):
     me = lax.axis_index("rows")
     k = me // 2
@@ -297,6 +297,8 @@
                 fc[par, len(NAMES) + n * CHUNK + m, lo:hi, :] = entry(e, m)
 
     def slot_of(r):
+        if isinstance(r, int):
+            return r + 16 if r < 4 else (r - 4 if r < 20 else r)
         return jnp.where(r < 4, r + 16, jnp.where(r < 20, r - 4, r))
 
     def line_group(par, it, rows):
@@ -345,6 +347,14 @@
                 total = term if total is None else total + term
             pb[it + 1, r, m] = total
 
+    def mass_row(it, n):
+        for m in range(CHUNK):
+            total = None
+            for e in range(9):
+                term = ce[(9 + e) * CHUNK + m, pl.ds(n + 4, 1), :] * zb[it, n + 7 + e // 3, m + e % 3]
+                total = term if total is None else total + term
+            mz[it, n, m] = total
+
     def send_halo(do):
         for n, (chip, at) in enumerate(((down, 8), (up, 12))):
             copy = pltpu.make_async_remote_copy(
@@ -428,11 +438,8 @@
             line_group(par, it, list(range(4 + it, 20 - it)))
             dots(it)
 
-            def rows(n, carry):
-                off_row(par, it, 5 + it + 2 * n)
-                off_row(par, it, 6 + it + 2 * n)
-                return carry
-            lax.fori_loop(0, 7 - it, rows, 0)
+            for r in range(5 + it, 19 - it):
+                off_row(par, it, r)
         dots(ITERS)
         stacked = jnp.concatenate([sums[pair] for pair in PAIRS] + [jnp.zeros((8, LANES), F32)], axis=0)
         packed = lax.dot_general(halves16, jnp.concatenate(split3(stacked), axis=0), (((1,), (1,)), ((), ())), preferred_element_type=F32)
@@ -485,6 +492,21 @@
                 return carry
             lax.fori_loop(0, ITERS, outer, 0)
 
+        @pl.when(t == STEPS - 1)
+        def _():
+            def images(n, carry):
+                mass_row(n // 4, 2 * (n % 4))
+                mass_row(n // 4, 2 * (n % 4) + 1)
+                return carry
+            lax.fori_loop(0, 4 * ITERS, images, 0)
+
+            def reorder(it, carry):
+                zn[it] = native(zb[it, 8:16, 1:CHUNK + 1])
+                zn[ITERS + it] = native(mz[it])
+                return carry
+            lax.fori_loop(0, ITERS, reorder, 0)
+            zn[2 * ITERS] = native(pb[0, 8:16])
+
         pltpu.make_async_copy(arb.at[t, pl.ds(0, chips - 1)], arb.at[t, pl.ds(0, chips - 1)], ar_recv.at[t]).wait()
         total = jnp.sum(arb[t], axis=0)
         total = jnp.concatenate([total] * 3 + [jnp.zeros((2, LANES), F32)], axis=0)
@@ -513,26 +535,61 @@
                     total = term if total is None else total + term
                 pb[0, r, m] = pb[0, r, m] - twice * total
             return carry
-        lax.fori_loop(7, 17, combine, 0, unroll=2)
-        lax.fori_loop(8, 16, update, 0, unroll=2)
+        @pl.when(t < STEPS - 1)
+        def _():
+            for r in range(7, 17):
+                combine(r, 0)
+            for r in range(8, 16):
+                update(r, 0)
 
         @pl.when(t == 0)
         def _():
             send_halo(lambda copy: copy.start())
 
-        @pl.when(t < 2)
-        def _():
-            lax.fori_loop(3, 7, combine, 0)
-            lax.fori_loop(17, 21, combine, 0)
-            lax.fori_loop(4, 8, update, 0, unroll=2)
-            lax.fori_loop(16, 20, update, 0, unroll=2)
+        @pl.when(t < STEPS - 1)
+        def _():
+            for r in list(range(3, 7)) + list(range(17, 21)):
+                combine(r, 0)
+            for r in list(range(4, 8)) + list(range(16, 20)):
+                update(r, 0)
+
+        @pl.when(t == STEPS - 1)
+        def _():
+            both = []
+            for value in y:
+                other = lane_roll(value, HALF)
+                both.append((jnp.where(left, value, other), jnp.where(left, other, value)))
+            scale = jnp.sqrt(jnp.full((8, LANES), twice, F32))
+
+            def weighted(base, factor, h, r, span):
+                total = (factor * both[0][h]) * zn[base, h, r, :, span]
+                for it in range(1, ITERS):
+                    total = total + (factor * both[it][h]) * zn[base + it, h, r, :, span]
+                return total
+
+            def low_row(r, carry):
+                for h in range(2):
+                    for q in range(4):
+                        span = slice(q * LANES, (q + 1) * LANES)
+                        os_[STEPS - 1, r, 8 * h:8 * h + 8, span] = weighted(0, scale, h, r, span)
+                return carry
+
+            def res_row(r, carry):
+                for h in range(2):
+                    for q in range(4):
+                        span = slice(q * LANES, (q + 1) * LANES)
+                        os_[STEPS, r, 8 * h:8 * h + 8, span] = zn[2 * ITERS, h, r, :, span] - weighted(ITERS, twice, h, r, span)
+                return carry
+            lax.fori_loop(0, 8, low_row, 0, unroll=2)
+            for copy in out_copies(STEPS - 1, out_ref(STEPS - 1)):
+                copy.start()
+            lax.fori_loop(0, 8, res_row, 0, unroll=2)
+            for copy in out_copies(STEPS, res_at):
+                copy.start()
         return carry
 
+    res_at = res_hbm.at[:, half_cols, :]
     lax.fori_loop(0, STEPS, adi, 0)
-
-    res_at = res_hbm.at[:, half_cols, :]
-    emit_low(STEPS - 1)
-    emit(STEPS, pb[0, 8:16], res_at)
 
     for copy in far_copies:
         copy.wait_send()
@@ -573,6 +630,8 @@
                 pltpu.VMEM((ITERS + 1,) + field, F32),
                 pltpu.VMEM((ITERS,) + framed, F32),
                 pltpu.VMEM(framed, F32),
+                pltpu.VMEM((ITERS, 8, CHUNK, 8, LANES), F32),
+                pltpu.VMEM((2 * ITERS + 1, 2, 8, 8, 512), F32),
                 pltpu.VMEM((STEPS + 1, 8, 16, 512), F32),
                 pltpu.VMEM((STEPS, chips, 2, LANES), F32),
                 pltpu.VMEM((2, 4, CHUNK, 8, LANES), F32),

time: 57.5 us -> 55.9 us (0.972)
  Pallas kernels: 53.9 us -> 52.3 us
    pallas_call x1, Pallas kernels: 53.9 us -> 52.3 us  [shards(): pl.pallas_call(functools.partial(kernel, chips), out_shape=(jax.ShapeDtyp...]
where the time goes in v5:
time: 55.9 us; the launch traced here: 55.7 us
  Pallas kernels  52.3 us (94%)
  local copies, waits for them, and re-layouts  2.81 us (5%)
  between operations  0.65 us (1%)
    pallas_call x1, Pallas kernels, shards(): pl.pallas_call(functools.partial(kernel, chips), out_shape=(jax.ShapeDtyp...  52.3 us
    unnamed x4, local copies, waits for them, and re-layouts  2.81 us

profile of v5, /device:TPU:1, one launch (start us, length us, event | category | flops | bytes accessed | tf_op | source)
XLA Modules:
  0.0 55.7 jit_solution(14165412593094025721)
XLA Ops:
  0.6 52.3 %shard_map.59 = (f32[3,4,32,512]{3,2,1,0:T(8,128)}, f32[4,32,512]{2,1,0:T(8,128)}) custom-call(f32[3]{0:T(128)} %shifts_hbm.1, f32[9,4,512]{2,1,0:T(4,128)} %stiff_hbm.1, f32[9,4,512]{2,1,0:T(4,128)} %mass_hbm.1, f32[4,32,512]{2,1,0:T(8,128)} %factor_hbm.1), custom_call_target="tpu_custom_call" | custom-call | tf_op jit(solution)/shard_map/pallas_call | solution.py:614
  52.9 0.0 copy-start
  52.9 2.1 %copy.8 = f32[3,4,32,512]{3,2,1,0:T(8,128)} copy(f32[3,4,32,512]{3,2,1,0:T(8,128)} %get-tuple-element.4) | data formatting | bytes 1572864
  55.0 0.0 copy-done
  55.0 0.7 %copy.9 = f32[4,32,512]{2,1,0:T(8,128)} copy(f32[4,32,512]{2,1,0:T(8,128)S(1)} %copy-done) | data formatting | bytes 524288
Async XLA Ops:
  52.9 2.1 %copy-start = (f32[4,32,512]{2,1,0:T(8,128)S(1)}, f32[4,32,512]{2,1,0:T(8,128)}, u32[]{:S(2)}) copy-start(f32[4,32,512]{2,1,0:T(8,128)} %get-tuple-element.5) | copy-start | bytes 786436

commit v6 on v5

--- a/solution.py
+++ b/solution.py
@@ -407,12 +407,10 @@
             wait_stencil(block)
     wait_stencil(1)
     wait_stencil(4)
+    for copy in far_copies:
+        copy.start()
     prepare((1, 2, 3, 4), 0)
     factor_rows(0, 0, 16)
-    for copy in near_copies:
-        copy.wait_send()
-    for copy in far_copies:
-        copy.start()
     for block in (2, 3):
         @pl.when(block == 3 - c)
         def _():
@@ -591,7 +589,7 @@
     res_at = res_hbm.at[:, half_cols, :]
     lax.fori_loop(0, STEPS, adi, 0)
 
-    for copy in far_copies:
+    for copy in near_copies + far_copies:
         copy.wait_send()
 
     def drain(t, carry):

time: 55.9 us -> 55.1 us (0.986)
  Pallas kernels: 52.3 us -> 51.5 us
    pallas_call x1, Pallas kernels: 52.3 us -> 51.5 us  [shards(): pl.pallas_call(functools.partial(kernel, chips), out_shape=(jax.ShapeDtyp...]
where the time goes in v6:
time: 55.1 us; the launch traced here: 54.9 us
  Pallas kernels  51.5 us (93%)
  local copies, waits for them, and re-layouts  2.81 us (5%)
  between operations  0.65 us (1%)
    pallas_call x1, Pallas kernels, shards(): pl.pallas_call(functools.partial(kernel, chips), out_shape=(jax.ShapeDtyp...  51.5 us
    unnamed x4, local copies, waits for them, and re-layouts  2.81 us

profile of v6, /device:TPU:1, one launch (start us, length us, event | category | flops | bytes accessed | tf_op | source)
XLA Modules:
  0.0 54.9 jit_solution(17739836057633288021)
XLA Ops:
  0.6 51.5 %shard_map.59 = (f32[3,4,32,512]{3,2,1,0:T(8,128)}, f32[4,32,512]{2,1,0:T(8,128)}) custom-call(f32[3]{0:T(128)} %shifts_hbm.1, f32[9,4,512]{2,1,0:T(4,128)} %stiff_hbm.1, f32[9,4,512]{2,1,0:T(4,128)} %mass_hbm.1, f32[4,32,512]{2,1,0:T(8,128)} %factor_hbm.1), custom_call_target="tpu_custom_call" | custom-call | tf_op jit(solution)/shard_map/pallas_call | solution.py:612
  52.1 0.0 copy-start
  52.1 2.1 %copy.8 = f32[3,4,32,512]{3,2,1,0:T(8,128)} copy(f32[3,4,32,512]{3,2,1,0:T(8,128)} %get-tuple-element.4) | data formatting | bytes 1572864
  54.2 0.0 copy-done
  54.2 0.7 %copy.9 = f32[4,32,512]{2,1,0:T(8,128)} copy(f32[4,32,512]{2,1,0:T(8,128)S(1)} %copy-done) | data formatting | bytes 524288
Async XLA Ops:
  52.1 2.1 %copy-start = (f32[4,32,512]{2,1,0:T(8,128)S(1)}, f32[4,32,512]{2,1,0:T(8,128)}, u32[]{:S(2)}) copy-start(f32[4,32,512]{2,1,0:T(8,128)} %get-tuple-element.5) | copy-start | bytes 786436
